TPU v7x, 32 devices: a whole 2x2x4 slice. The times are simulated.
32 devices in a mesh: groups: 2 (over x), blk: 16 (over z, y, core).
Axes of the slice: x: 2, y: 2, z: 4, core: 2. Of those that a mesh axis runs over, the one named last changes fastest.
Arguments:
- frames: bfloat16 [256, 16384], P(('groups', 'blk')), parts along dimension 0
- basis: bfloat16 [256, 64], P(('groups', 'blk')), parts along dimension 0, may hold values from -6 to 6
- density: bfloat16 [256], P(('groups', 'blk')), parts along dimension 0, may hold values from 0.25 to 4
Outputs:
- residual_block: bfloat16 [256, 64], P(('groups', 'blk')), parts along dimension 0
- coefficients: float32 [128, 64], P('groups'), parts along dimension 0
There are 2 independent parts, one for each index of `groups`. A program takes and returns all parts, laid end to end along the dimension named above; each array names one. Nothing has to cross between parts.
All inputs are finite; a program needn't handle non-finite values.
Results may differ from a plain program's by a relative error of at most 0.0045.
Values may be sent and summed in bfloat16 or wider, within the bound.
No kernel may reach another device: no remote copies, remote signals or barrier semaphores. Data moves between devices by JAX's collectives and lax.ppermute only.
A program may use at most 64 MiB of HBM per device.

v0:
```python
import jax
import jax.numpy as jnp
from jax import lax
from jax.sharding import PartitionSpec as P


def pair_kernel(left, left_norms, right):
    right_norms = jnp.sum(jnp.square(right.astype(jnp.float32)), axis=1)
    inner_products = lax.dot_general(
        left, right, (((1,), (1,)), ((), ())), preferred_element_type=jnp.float32
    )
    squared_dist = left_norms[:, None] + right_norms[None, :] - 2.0 * inner_products
    return jnp.exp(-squared_dist / left.shape[1])


def shards(frames, basis, density):
    own_norms = jnp.sum(jnp.square(frames.astype(jnp.float32)), axis=1)
    row_count = frames.shape[0]
    blocks = lax.all_gather(frames, "blk", axis=0, tiled=True)
    vectors = lax.all_gather(basis, "blk", axis=0, tiled=True)
    weights_in = lax.all_gather(density, "blk", axis=0, tiled=True)
    kernel = pair_kernel(frames, own_norms, blocks)
    forward = (kernel * weights_in.astype(jnp.float32)[None, :]).astype(jnp.bfloat16)
    numer = jnp.dot(forward, vectors, preferred_element_type=jnp.float32)
    totals = jnp.sum(forward.astype(jnp.float32), axis=1)
    numer, totals = (numer, totals)
    applied = numer / totals[:, None]
    basis_f = basis.astype(jnp.float32)
    local_coef = lax.dot_general(
        basis_f,
        applied,
        (((0,), (0,)), ((), ())),
        precision=lax.Precision.HIGHEST,
        preferred_element_type=jnp.float32,
    )
    coefficients = lax.psum(local_coef, "blk")
    frame_total = row_count * lax.axis_size("blk")
    projection = jnp.dot(
        basis_f, coefficients, precision=lax.Precision.HIGHEST, preferred_element_type=jnp.float32
    )
    residual_block = (applied - projection / frame_total).astype(jnp.bfloat16)
    return (residual_block, coefficients)


def solution(mesh):
    placed = (P(("groups", "blk"), None), P(("groups", "blk"), None), P(("groups", "blk")))
    return jax.shard_map(
        shards,
        mesh=mesh,
        in_specs=placed,
        out_specs=(P(("groups", "blk"), None), P("groups", None)),
        check_vma=False,
    )
```

profile of v0, /device:TPU:0, one launch (start us, length us, event | category | flops | bytes accessed | tf_op | source)
XLA Modules:
  0.0 137.7 jit_solution(3754534518135585667)
XLA Ops:
  7.2 0.0 copy-start.1
  7.2 0.0 all-gather.2.cloned.1.call-start
  7.2 0.7 all-gather.2.cloned.1.call-update
  7.9 1.2 dynamic-slice
  9.8 0.9 dynamic-update-slice
  10.7 35.4 %all-reduce = bf16[128]{0:T(256)(128)(2,1)S(1)} all-reduce(bf16[128]{0:T(256)(128)(2,1)S(1)} %dynamic-update-slice), channel_id=1, replica_groups=mesh['groups'=2,'blk'=16] {'blk'}, use_global_device_ids=true, to_apply=%add | all-reduce | flops 128 | bytes 512
  46.1 17.6 %all_gather.11 = bf16[128,64]{1,0:T(8,128)(2,1)S(1)} all-gather(bf16[8,64]{1,0:T(8,128)(2,1)} %param.4), channel_id=1, replica_groups=mesh['groups'=2,'blk'=16] {'blk'}, dimensions={0}, use_global_device_ids=true | all-gather | bytes 17408 | tf_op jit(solution)/shard_map/all_gather | solution.py:20
  63.7 1.2 multiply_reduce_fusion.1
  64.9 0.0 all-gather.2.cloned.1.call-done
  64.9 0.0 copy-start
  64.9 0.0 copy-start.2
  64.9 3.2 %multiply_reduce_fusion = f32[128]{0:T(128)S(1)} fusion(bf16[128,16384]{1,0:T(8,128)(2,1)} %all-gather.2.cloned.1.call-done), kind=kLoop, calls=%fused_computation | loop fusion | flops 6291328 | bytes 4194816 | tf_op jit(solution)/shard_map/reduce_sum | solution.py:8
  68.2 0.0 copy-done.1
  68.2 0.2 copy-done
  68.4 1.3 convert_reduce_fusion
  69.7 0.1 convolution_divide_fusion
  69.8 0.0 copy-done.2
  69.8 0.2 convolution_bitcast_fusion
  70.0 59.3 %psum.7 = f32[64,64]{0,1:T(8,128)S(1)} all-reduce(f32[64,64]{0,1:T(8,128)S(1)} %convolution_bitcast_fusion), channel_id=1, replica_groups=mesh['groups'=2,'blk'=16] {'blk'}, use_global_device_ids=true, to_apply=%region_3.0 | all-reduce | flops 4096 | bytes 32768 | tf_op jit(solution)/shard_map/psum | solution.py:36
  129.4 0.7 fusion.8
  130.1 0.7 copy.5
  (2 shorter events, 0.0 us)
Async XLA Ops:
  7.2 61.0 %copy-start.1 = (bf16[8,16384]{1,0:T(8,128)(2,1)S(1)}, bf16[8,16384]{1,0:T(8,128)(2,1)}, u32[]{:S(2)}) copy-start(bf16[8,16384]{1,0:T(8,128)(2,1)} %param.3) | copy-start | bytes 786436
  7.2 57.7 %all-gather.2.cloned.1.call-start = ((), (), s32[]{:S(2)}) async-start(), calls=%async_computation | async-start | bytes 4456448 | tf_op jit(solution)/shard_map/all_gather | solution.py:19
  64.9 3.5 %copy-start = (bf16[128,16384]{1,0:T(8,128)(2,1)S(1)}, bf16[128,16384]{1,0:T(8,128)(2,1)}, u32[]{:S(2)}) copy-start(bf16[128,16384]{1,0:T(8,128)(2,1)} %all-gather.2.cloned.1.call-done) | copy-start | bytes 12582916
  64.9 4.9 %copy-start.2 = (bf16[8,64]{1,0:T(8,128)(2,1)S(1)}, bf16[8,64]{1,0:T(8,128)(2,1)}, u32[]{:S(2)}) copy-start(bf16[8,64]{1,0:T(8,128)(2,1)} %param.4) | copy-start | bytes 3076
Sparse Core Ops, SparseCore 0:
  10.2 53.5 all-gather.1
where the time goes:
time: 138 us
  blocking collectives  112 us (81%)
  between operations  14.7 us (11%)
  other arithmetic  4.43 us (3%)
  local copies, waits for them, and re-layouts  3.01 us (2%)
  matrix products  2.4 us (2%)
    psum x1, blocking collectives, shards(): coefficients = lax.psum(local_coef, 'blk')  59.3 us
    unnamed x1, blocking collectives  35.4 us
    all_gather x1, blocking collectives, shards(): vectors = lax.all_gather(basis, 'blk', axis=0, tiled=True)  17.6 us
    reduce_sum x1, other arithmetic, pair_kernel(): right_norms = jnp.sum(jnp.square(right.astype(jnp.float32)), axis=1)  3.23 us
    unnamed x10, local copies, waits for them, and re-layouts  3.01 us
  transfers between devices with their start and end apart: 1, of which 0 were waited for; matrix products, arithmetic and copies ran while one was open for 2% of the time, Pallas kernels for 0%

commit v1 on v0

v1 whole, which is shorter than its diff:
```python
import functools

import jax
import jax.numpy as jnp
from jax import lax
from jax.experimental import pallas as pl
from jax.experimental.pallas import tpu as pltpu
from jax.sharding import PartitionSpec as P


def partial_kernel(count, features_ref, basis_ref, density_ref, message_ref):
    features = features_ref[...]
    total = features.shape[0]
    half = total // 2
    rows, width = basis_ref.shape
    inner = lax.dot_general(
        features, features, (((1,), (1,)), ((), ())), preferred_element_type=jnp.float32
    )
    row = lax.broadcasted_iota(jnp.int32, (total, total), 0)
    lane = lax.broadcasted_iota(jnp.int32, (total, total), 1)
    diagonal = jnp.where(row == lane, inner, 0.0)
    dist = (
        jnp.sum(diagonal, axis=1, keepdims=True)
        + jnp.sum(diagonal, axis=0, keepdims=True)
        - 2.0 * inner
    )
    top, bottom = dist[:half], pltpu.roll(dist[half:], half, 1)
    own_row, own_lane = row[:half], lane[:half]
    packed = jnp.where((own_lane < half) & (own_row >= own_lane), bottom, top)

    me = lax.axis_index("blk")
    vectors = jnp.concatenate(
        [
            basis_ref[...].astype(jnp.float32),
            jnp.ones((rows, 1), jnp.float32),
            jnp.zeros((rows, total - width - 1), jnp.float32),
        ],
        axis=1,
    )
    density = density_ref[...].astype(jnp.float32).reshape(1, rows)
    spread = jnp.concatenate([density, jnp.zeros((1, total - rows), jnp.float32)], axis=1)
    spread = pltpu.roll(jnp.broadcast_to(spread, (rows, total)), me * rows, 1)
    message = jnp.concatenate([packed, vectors, spread], axis=0).astype(jnp.bfloat16)
    for peer in range(count):
        message_ref[peer] = message


def finish_kernel(count, feature_count, rows, width, received_ref, residual_ref, coef_ref, applied_ref):
    total = count * rows
    half = total // 2
    packed = received_ref[0, :half].astype(jnp.float32)
    density = received_ref[0, half:].astype(jnp.float32)[rows : rows + 1]
    for peer in range(1, count):
        packed += received_ref[peer, :half].astype(jnp.float32)
        density += received_ref[peer, half:].astype(jnp.float32)[rows : rows + 1]
    row = lax.broadcasted_iota(jnp.int32, (half, total), 0)
    lane = lax.broadcasted_iota(jnp.int32, (half, total), 1)
    top = jnp.where((lane >= half) | (row < lane), packed, 0.0)
    bottom = pltpu.roll(jnp.where((lane < half) & (row > lane), packed, 0.0), half, 1)
    one_side = jnp.concatenate([top, bottom], axis=0)
    dist = one_side + one_side.T
    weight = (jnp.exp(-dist / feature_count) * density).astype(jnp.bfloat16)
    vectors = jnp.concatenate(
        [received_ref[peer, half:].astype(jnp.float32)[:rows, :128] for peer in range(count)], axis=0
    )
    numer = jnp.dot(weight, vectors.astype(jnp.bfloat16), preferred_element_type=jnp.float32)
    applied = numer[:, :width] / numer[:, width : width + 1]
    applied_ref[...] = applied
    coef = lax.dot_general(
        vectors[:, :width],
        applied,
        (((0,), (0,)), ((), ())),
        precision=lax.Precision.HIGHEST,
        preferred_element_type=jnp.float32,
    )
    coef_ref[...] = coef
    me = lax.axis_index("blk")
    own = received_ref[me, half:].astype(jnp.float32)[:rows, :width]
    projection = jnp.dot(
        own, coef, precision=lax.Precision.HIGHEST, preferred_element_type=jnp.float32
    )
    own_applied = applied_ref[pl.ds(pl.multiple_of(me * rows, rows), rows), :]
    residual_ref[...] = (own_applied - projection / total).astype(jnp.bfloat16)


def shards(frames, basis, density):
    count = lax.axis_size("blk")
    rows, feature_count = frames.shape
    width = basis.shape[1]
    total = rows * count
    whole = pl.BlockSpec(memory_space=pltpu.VMEM)
    params = pltpu.CompilerParams(vmem_limit_bytes=48 << 20)
    features = lax.all_to_all(frames, "blk", split_axis=1, concat_axis=0, tiled=True)
    message = pl.pallas_call(
        functools.partial(partial_kernel, count),
        out_shape=jax.ShapeDtypeStruct((count, total // 2 + 2 * rows, total), jnp.bfloat16),
        in_specs=[whole] * 3,
        out_specs=whole,
        compiler_params=params,
    )(features, basis, density)
    received = lax.all_to_all(message, "blk", split_axis=0, concat_axis=0, tiled=True)
    return pl.pallas_call(
        functools.partial(finish_kernel, count, feature_count, rows, width),
        out_shape=(
            jax.ShapeDtypeStruct((rows, width), jnp.bfloat16),
            jax.ShapeDtypeStruct((width, width), jnp.float32),
        ),
        in_specs=[whole],
        out_specs=(whole, whole),
        scratch_shapes=[pltpu.VMEM((total, width), jnp.float32)],
        compiler_params=params,
    )(received)


def solution(mesh):
    placed = (P(("groups", "blk"), None), P(("groups", "blk"), None), P(("groups", "blk")))
    return jax.shard_map(
        shards,
        mesh=mesh,
        in_specs=placed,
        out_specs=(P(("groups", "blk"), None), P("groups", None)),
        check_vma=False,
    )
```

time: 138 us -> 34.6 us (0.25)
  blocking collectives: 112 us -> 31.3 us
  between operations: 14.7 us -> 0.65 us
  other arithmetic: 4.43 us -> 0 us
  matrix products: 2.4 us -> 0 us
  local copies, waits for them, and re-layouts: 3.01 us -> 0.66 us
  Pallas kernels: 0 us -> 1.72 us
    psum x1 -> x0, blocking collectives: 59.3 us -> none  [shards(): coefficients = lax.psum(local_coef, 'blk')]
    unnamed x1 -> x0, blocking collectives: 35.4 us -> none
    all_to_all x0 -> x2, blocking collectives: none -> 31.3 us  [the longest x1 17.4 us: shards(): lax.all_to_all(frames, 'blk', split_axis=1, concat_axis=0, tiled=True)]
    all_gather x1 -> x0, blocking collectives: 17.6 us -> none  [shards(): vectors = lax.all_gather(basis, 'blk', axis=0, tiled=True)]
    reduce_sum x2 -> x0, other arithmetic: 4.43 us -> none  [the longest x1 3.23 us: pair_kernel(): right_norms = jnp.sum(jnp.square(right.astype(jnp.float32)), axis=1)]
    dot_general x4 -> x0, matrix products: 2.4 us -> none  [the longest x1 1.3 us: pair_kernel(): lax.dot_general(left, right, (((1,), (1,)), ((), ())), preferred_element_...]
    unnamed x10 -> x4, local copies, waits for them, and re-layouts: 3.01 us -> 0.66 us
    pallas_call x0 -> x2, Pallas kernels: none -> 1.72 us  [the longest x1 1.34 us: shards(): pl.pallas_call(functools.partial(finish_kernel, count, feature_count, row...]
  transfers between devices with their start and end apart: 1 -> 0, of which waited for: 0 -> 0; matrix products, arithmetic and copies ran while one was open for 2% -> 0% of each run, Pallas kernels for 0% -> 0%
where the time goes in v1:
time: 34.6 us; the launch traced here: 34.3 us
  blocking collectives  31.3 us (90%)
  Pallas kernels  1.72 us (5%)
  local copies, waits for them, and re-layouts  0.66 us (2%)
  between operations  0.65 us (2%)
    all_to_all x1, blocking collectives, shards(): lax.all_to_all(frames, 'blk', split_axis=1, concat_axis=0, tiled=True)  17.4 us
    all_to_all x1, blocking collectives, shards(): lax.all_to_all(message, 'blk', split_axis=0, concat_axis=0, tiled=True)  13.9 us
    pallas_call x1, Pallas kernels, shards(): pl.pallas_call(functools.partial(finish_kernel, count, feature_count, row...  1.34 us

profile of v1, /device:TPU:0, one launch (start us, length us, event | category | flops | bytes accessed | tf_op | source)
XLA Modules:
  0.0 34.3 jit_solution(1880877275340880906)
XLA Ops:
  0.6 0.0 copy-start
  0.6 17.4 %all_to_all.24 = bf16[8,16,1024]{2,0,1:T(8,128)(2,1)S(1)} all-to-all(bf16[8,16,1024]{2,0,1:T(8,128)(2,1)} %bitcast.5), channel_id=1, replica_groups=mesh['groups'=2,'blk'=16] {'blk'}, dimensions={1} | all-to-all | bytes 524288 | tf_op jit(solution)/shard_map/all_to_all | solution.py:93
  18.1 0.0 copy-start.1
  18.1 0.0 copy-done
  18.1 0.7 %copy-done.1 = bf16[8]{0:T(256)(128)(2,1)S(1)} copy-done((bf16[8]{0:T(256)(128)(2,1)S(1)}, bf16[8]{0:T(256)(128)(2,1)}, u32[]{:S(2)}) %copy-start.1) | copy-done | bytes 40
  18.7 0.4 %shard_map.50 = bf16[16,80,128]{2,1,0:T(8,128)(2,1)S(1)} custom-call(bf16[128,1024]{1,0:T(8,128)(2,1)S(1)} %bitcast.4, bf16[8,64]{1,0:T(8,128)(2,1)S(1)} %copy-done, bf16[8]{0:T(256)(128)(2,1)S(1)} %copy-done.1), custom_call_target="tpu_custom_call" | custom-call | tf_op jit(solution)/shard_map/pallas_call | solution.py:94
  19.1 13.9 %all_to_all.25.received_ref = bf16[16,80,128]{2,1,0:T(8,128)(2,1)S(1)} all-to-all(bf16[16,80,128]{2,1,0:T(8,128)(2,1)S(1)} %shard_map.50), channel_id=1, replica_groups=mesh['groups'=2,'blk'=16] {'blk'}, dimensions={0} | all-to-all | bytes 655360 | tf_op jit(solution)/shard_map/all_to_all | solution.py:101
  33.0 1.3 %shard_map.51 = (bf16[8,64]{1,0:T(8,128)(2,1)}, f32[64,64]{1,0:T(8,128)}) custom-call(bf16[16,80,128]{2,1,0:T(8,128)(2,1)S(1)} %all_to_all.25.received_ref), custom_call_target="tpu_custom_call" | custom-call | tf_op jit(solution)/shard_map/pallas_call | solution.py:102
Async XLA Ops:
  0.6 17.5 %copy-start = (bf16[8,64]{1,0:T(8,128)(2,1)S(1)}, bf16[8,64]{1,0:T(8,128)(2,1)}, u32[]{:S(2)}) copy-start(bf16[8,64]{1,0:T(8,128)(2,1)} %basis_ref.1) | copy-start | bytes 3076
  18.1 0.7 %copy-start.1 = (bf16[8]{0:T(256)(128)(2,1)S(1)}, bf16[8]{0:T(256)(128)(2,1)}, u32[]{:S(2)}) copy-start(bf16[8]{0:T(256)(128)(2,1)} %density_ref.1) | copy-start | bytes 52

commit v2 on v1

v2 whole, which is shorter than its diff:
```python
import functools

import jax
import jax.numpy as jnp
from jax import lax
from jax.experimental import pallas as pl
from jax.experimental.pallas import tpu as pltpu
from jax.sharding import PartitionSpec as P


def partial_kernel(features_ref, basis_ref, density_ref, message_ref):
    features = features_ref[...]
    total = features.shape[0]
    half = total // 2
    rows, width = basis_ref.shape
    inner = lax.dot_general(
        features, features, (((1,), (1,)), ((), ())), preferred_element_type=jnp.float32
    )
    row = lax.broadcasted_iota(jnp.int32, (total, total), 0)
    lane = lax.broadcasted_iota(jnp.int32, (total, total), 1)
    diagonal = jnp.where(row == lane, inner, 0.0)
    dist = (
        jnp.sum(diagonal, axis=1, keepdims=True)
        + jnp.sum(diagonal, axis=0, keepdims=True)
        - 2.0 * inner
    )
    top, bottom = dist[:half], pltpu.roll(dist[half:], half, 1)
    own_row, own_lane = row[:half], lane[:half]
    packed = jnp.where((own_lane < half) & (own_row >= own_lane), bottom, top)

    me = lax.axis_index("blk")
    density = density_ref[...].astype(jnp.float32).reshape(1, rows)
    density = jnp.concatenate([density, jnp.zeros((1, total - rows), jnp.float32)], axis=1)
    density = pltpu.roll(density, lax.rem(me * rows, half), 1)
    packed = jnp.where(own_row == own_lane, density, packed)
    vectors = jnp.concatenate(
        [basis_ref[...].astype(jnp.float32), jnp.zeros((rows, total - width), jnp.float32)], axis=1
    )
    message_ref[:half] = packed
    message_ref[half:] = pltpu.roll(vectors, lax.rem(me, 2) * width, 1)


def finish_kernel(feature_count, width, received_ref, residual_ref, coef_ref, applied_ref, vectors_ref):
    pairs, height, total = received_ref.shape
    half = total // 2
    rows = height - half
    first = sum(received_ref[pair, :half].astype(jnp.float32) for pair in range(pairs // 2))
    second = sum(received_ref[pair, :half].astype(jnp.float32) for pair in range(pairs // 2, pairs))
    packed = first + second
    row = lax.broadcasted_iota(jnp.int32, (half, total), 0)
    lane = lax.broadcasted_iota(jnp.int32, (half, total), 1)
    slots = jnp.where(row == lane, first, 0.0) + pltpu.roll(
        jnp.where(row == lane, second, 0.0), half, 1
    )
    density = jnp.sum(slots, axis=0, keepdims=True)
    top = jnp.where((lane >= half) | (row < lane), packed, 0.0)
    bottom = pltpu.roll(jnp.where((lane < half) & (row > lane), packed, 0.0), half, 1)
    one_side = jnp.concatenate([top, bottom], axis=0)
    dist = one_side + one_side.T
    weight = (jnp.exp(-dist / feature_count) * density).astype(jnp.bfloat16)
    for pair in range(pairs):
        both = received_ref[pair, half:].astype(jnp.float32)
        vectors_ref[2 * pair * rows : (2 * pair + 1) * rows] = both[:, :width]
        vectors_ref[(2 * pair + 1) * rows : (2 * pair + 2) * rows] = both[:, width : 2 * width]
    vectors = vectors_ref[...]
    extended = jnp.concatenate(
        [vectors, jnp.ones((total, 1), jnp.float32), jnp.zeros((total, width - 1), jnp.float32)], axis=1
    )
    numer = jnp.dot(weight, extended.astype(jnp.bfloat16), preferred_element_type=jnp.float32)
    applied = numer[:, :width] / numer[:, width : width + 1]
    applied_ref[...] = applied
    coef = lax.dot_general(
        vectors,
        applied,
        (((0,), (0,)), ((), ())),
        precision=lax.Precision.HIGHEST,
        preferred_element_type=jnp.float32,
    )
    coef_ref[...] = coef
    me = lax.axis_index("blk")
    own_rows = pl.ds(pl.multiple_of(me * rows, rows), rows)
    projection = jnp.dot(
        vectors_ref[own_rows, :],
        coef,
        precision=lax.Precision.HIGHEST,
        preferred_element_type=jnp.float32,
    )
    residual_ref[...] = (applied_ref[own_rows, :] - projection / total).astype(jnp.bfloat16)


def shards(frames, basis, density):
    count = lax.axis_size("blk")
    rows, feature_count = frames.shape
    width = basis.shape[1]
    total = rows * count
    whole = pl.BlockSpec(memory_space=pltpu.VMEM)
    params = pltpu.CompilerParams(vmem_limit_bytes=48 << 20)
    features = lax.all_to_all(frames, "blk", split_axis=1, concat_axis=0, tiled=True)
    partial = pl.pallas_call(
        partial_kernel,
        out_shape=jax.ShapeDtypeStruct((total // 2 + rows, total), jnp.float32),
        in_specs=[whole] * 3,
        out_specs=whole,
        compiler_params=params,
    )(features, basis, density)
    partial += lax.ppermute(partial, "blk", [(i, i ^ 1) for i in range(count)])
    pairs = count // 2
    message = jnp.broadcast_to(partial.astype(jnp.bfloat16), (pairs, *partial.shape))
    received = lax.all_to_all(
        message,
        "blk",
        split_axis=0,
        concat_axis=0,
        tiled=True,
        axis_index_groups=[list(range(core, count, 2)) for core in range(2)],
    )
    return pl.pallas_call(
        functools.partial(finish_kernel, feature_count, width),
        out_shape=(
            jax.ShapeDtypeStruct((rows, width), jnp.bfloat16),
            jax.ShapeDtypeStruct((width, width), jnp.float32),
        ),
        in_specs=[whole],
        out_specs=(whole, whole),
        scratch_shapes=[pltpu.VMEM((total, width), jnp.float32)] * 2,
        compiler_params=params,
    )(received)


def solution(mesh):
    placed = (P(("groups", "blk"), None), P(("groups", "blk"), None), P(("groups", "blk")))
    return jax.shard_map(
        shards,
        mesh=mesh,
        in_specs=placed,
        out_specs=(P(("groups", "blk"), None), P("groups", None)),
        check_vma=False,
    )
```

time: 34.6 us -> 32.3 us (0.934)
  blocking collectives: 31.3 us -> 27.7 us
  waiting for transfers between devices: 0 us -> 1.2 us
    all_to_all x1, blocking collectives: 13.9 us -> 10.2 us  [shards(): lax.all_to_all(message, 'blk', split_axis=0, concat_axis=0, tiled=True, a...]
    ppermute x0 -> x1, waiting for transfers between devices: none -> 1.2 us  [shards(): partial += lax.ppermute(partial, 'blk', [(i, i ^ 1) for i in range(count)])]
  transfers between devices with their start and end apart: 0 -> 1, of which waited for: 0 -> 1; matrix products, arithmetic and copies ran while one was open for 0% -> 0% of each run, Pallas kernels for 0% -> 0%
where the time goes in v2:
time: 32.3 us; the launch traced here: 32 us
  blocking collectives  27.7 us (86%)
  Pallas kernels  1.69 us (5%)
  waiting for transfers between devices  1.2 us (4%)
  local copies, waits for them, and re-layouts  0.68 us (2%)
  between operations  0.67 us (2%)
    all_to_all x1, blocking collectives, shards(): lax.all_to_all(frames, 'blk', split_axis=1, concat_axis=0, tiled=True)  17.4 us
    all_to_all x1, blocking collectives, shards(): lax.all_to_all(message, 'blk', split_axis=0, concat_axis=0, tiled=True, a...  10.2 us
    pallas_call x1, Pallas kernels, shards(): pl.pallas_call(functools.partial(finish_kernel, feature_count, width), ou...  1.32 us
    ppermute x1, waiting for transfers between devices, shards(): partial += lax.ppermute(partial, 'blk', [(i, i ^ 1) for i in range(count)])  1.2 us
    unnamed x4, local copies, waits for them, and re-layouts  0.66 us
  transfers between devices with their start and end apart: 1, of which 1 were waited for; matrix products, arithmetic and copies ran while one was open for 0% of the time, Pallas kernels for 0%

profile of v2, /device:TPU:0, one launch (start us, length us, event | category | flops | bytes accessed | tf_op | source)
XLA Modules:
  0.0 32.0 jit_solution(14541554074544104967)
XLA Ops:
  0.6 0.0 copy-start
  0.6 17.4 %all_to_all.24 = bf16[8,16,1024]{2,0,1:T(8,128)(2,1)S(1)} all-to-all(bf16[8,16,1024]{2,0,1:T(8,128)(2,1)} %bitcast.5), channel_id=1, replica_groups=mesh['groups'=2,'blk'=16] {'blk'}, dimensions={1} | all-to-all | bytes 524288 | tf_op jit(solution)/shard_map/all_to_all | solution.py:98
  18.1 0.0 copy-start.1
  18.1 0.0 copy-done
  18.1 0.7 %copy-done.1 = bf16[8]{0:T(256)(128)(2,1)S(1)} copy-done((bf16[8]{0:T(256)(128)(2,1)S(1)}, bf16[8]{0:T(256)(128)(2,1)}, u32[]{:S(2)}) %copy-start.1) | copy-done | bytes 40
  18.7 0.4 %shard_map.50 = f32[72,128]{1,0:T(8,128)S(1)} custom-call(bf16[128,1024]{1,0:T(8,128)(2,1)S(1)} %bitcast.4, bf16[8,64]{1,0:T(8,128)(2,1)S(1)} %copy-done, bf16[8]{0:T(256)(128)(2,1)S(1)} %copy-done.1), custom_call_target="tpu_custom_call" | custom-call | tf_op jit(solution)/shard_map/pallas_call | solution.py:99
  19.1 0.1 collective-permute-start
  19.2 1.2 %collective-permute-done = f32[72,128]{1,0:T(8,128)S(1)} collective-permute-done((f32[72,128]{1,0:T(8,128)S(1)}, f32[72,128]{1,0:T(8,128)S(1)}, u32[]{:S(2)}, u32[]{:S(2)}) %collective-permute-start) | collective-permute-done | bytes 36896 | tf_op jit(solution)/shard_map/ppermute | solution.py:106
  20.4 10.2 %all_to_all.25.received_ref = bf16[8,72,128]{2,1,0:T(8,128)(2,1)S(1)} all-to-all(bf16[8,72,128]{2,1,0:T(8,128)(2,1)S(1)} %broadcast_in_dim.3), channel_id=1, replica_groups={{0,2,4,6,8,10,12,14},{1,3,5,7,9,11,13,15},{16,18,20,22,24,26,28,30},{17..., dimensions={0} | all-to-all | bytes 294912 | tf_op jit(solution)/shard_map/all_to_all | solution.py:109
  30.7 1.3 %shard_map.51 = (bf16[8,64]{1,0:T(8,128)(2,1)}, f32[64,64]{1,0:T(8,128)}) custom-call(bf16[8,72,128]{2,1,0:T(8,128)(2,1)S(1)} %all_to_all.25.received_ref), custom_call_target="tpu_custom_call" | custom-call | tf_op jit(solution)/shard_map/pallas_call | solution.py:117
  (2 shorter events, 0.0 us)
Async XLA Ops:
  0.6 17.5 %copy-start = (bf16[8,64]{1,0:T(8,128)(2,1)S(1)}, bf16[8,64]{1,0:T(8,128)(2,1)}, u32[]{:S(2)}) copy-start(bf16[8,64]{1,0:T(8,128)(2,1)} %basis_ref.1) | copy-start | bytes 3076
  18.1 0.7 %copy-start.1 = (bf16[8]{0:T(256)(128)(2,1)S(1)}, bf16[8]{0:T(256)(128)(2,1)}, u32[]{:S(2)}) copy-start(bf16[8]{0:T(256)(128)(2,1)} %density_ref.1) | copy-start | bytes 52
  19.1 1.3 %collective-permute-start = (f32[72,128]{1,0:T(8,128)S(1)}, f32[72,128]{1,0:T(8,128)S(1)}, u32[]{:S(2)}, u32[]{:S(2)}) collective-permute-start(f32[72,128]{1,0:T(8,128)S(1)} %shard_map.50), channel_id=1, source_target_pairs={{0,1},{1,0},{2,3},{3,2},{4,5},{5,4},{6,7},{7,6},{8,9},{9,8},{10,11... | collective-permute-start | bytes 110600 | tf_op jit(solution)/shard_map/ppermute | solution.py:106

commit v3 on v2

v3 whole, which is shorter than its diff:
```python
import functools

import jax
import jax.numpy as jnp
from jax import lax
from jax.experimental import pallas as pl
from jax.experimental.pallas import tpu as pltpu
from jax.sharding import PartitionSpec as P

PLANE = 4


def partial_kernel(features_ref, basis_hbm, density_hbm, message_ref, basis_ref, density_ref, sems):
    copies = [
        pltpu.make_async_copy(basis_hbm, basis_ref, sems.at[0]),
        pltpu.make_async_copy(density_hbm, density_ref, sems.at[1]),
    ]
    for copy in copies:
        copy.start()
    features = features_ref[...]
    total = features.shape[0]
    half = total // 2
    rows, width = basis_ref.shape
    inner = lax.dot_general(
        features, features, (((1,), (1,)), ((), ())), preferred_element_type=jnp.float32
    )
    row = lax.broadcasted_iota(jnp.int32, (total, total), 0)
    lane = lax.broadcasted_iota(jnp.int32, (total, total), 1)
    diagonal = jnp.where(row == lane, inner, 0.0)
    dist = (
        jnp.sum(diagonal, axis=1, keepdims=True)
        + jnp.sum(diagonal, axis=0, keepdims=True)
        - 2.0 * inner
    )
    top, bottom = dist[:half], pltpu.roll(dist[half:], half, 1)
    own_row, own_lane = row[:half], lane[:half]
    packed = jnp.where((own_lane < half) & (own_row >= own_lane), bottom, top)

    for copy in copies:
        copy.wait()
    me = lax.axis_index("blk")
    density = density_ref[...].astype(jnp.float32).reshape(1, rows)
    density = jnp.concatenate([density, jnp.zeros((1, total - rows), jnp.float32)], axis=1)
    density = pltpu.roll(density, lax.rem(me * rows, half), 1)
    message_ref[:half] = jnp.where(own_row == own_lane, density, packed)
    place = lax.rem(me, PLANE)
    vectors = jnp.concatenate(
        [basis_ref[...].astype(jnp.float32), jnp.zeros((rows, total - width), jnp.float32)], axis=1
    )
    vectors = pltpu.roll(vectors, lax.rem(place, 2) * width, 1)
    message_ref[half : half + rows] = jnp.where(place < 2, vectors, 0.0)
    message_ref[half + rows :] = jnp.where(place < 2, 0.0, vectors)


def finish_kernel(feature_count, width, rows, *refs):
    planes = len(refs) - 4
    message_refs = refs[:planes]
    residual_ref, coef_ref, applied_ref, vectors_ref = refs[planes:]
    total = message_refs[0].shape[1]
    half = total // 2
    me = lax.axis_index("blk")
    plane = lax.div(me, PLANE)
    near = sum(ref[:half].astype(jnp.float32) for ref in message_refs[: planes // 2])
    far = sum(ref[:half].astype(jnp.float32) for ref in message_refs[planes // 2 :])
    packed = near + far
    row = lax.broadcasted_iota(jnp.int32, (half, total), 0)
    lane = lax.broadcasted_iota(jnp.int32, (half, total), 1)
    slots = [
        jnp.sum(jnp.where(row == lane, part, 0.0), axis=0, keepdims=True) for part in (near, far)
    ]
    upper = lax.div(plane, planes // 2)
    density = pltpu.roll(slots[0], upper * half, 1) + pltpu.roll(slots[1], (1 - upper) * half, 1)
    top = jnp.where((lane >= half) | (row < lane), packed, 0.0)
    bottom = pltpu.roll(jnp.where((lane < half) & (row > lane), packed, 0.0), half, 1)
    one_side = jnp.concatenate([top, bottom], axis=0)
    dist = one_side + one_side.T
    weight = (jnp.exp(-dist / feature_count) * density).astype(jnp.bfloat16)
    for offset, ref in enumerate(message_refs):
        tail = ref[half:].astype(jnp.float32)
        base = (plane ^ offset) * PLANE * rows
        for place in range(PLANE):
            block = tail[place // 2 * rows :][:rows, place % 2 * width :][:, :width]
            vectors_ref[pl.ds(pl.multiple_of(base + place * rows, rows), rows), :] = block
    vectors = vectors_ref[...]
    extended = jnp.concatenate(
        [vectors, jnp.ones((total, 1), jnp.float32), jnp.zeros((total, width - 1), jnp.float32)], axis=1
    )
    numer = jnp.dot(weight, extended.astype(jnp.bfloat16), preferred_element_type=jnp.float32)
    applied = numer[:, :width] / numer[:, width : width + 1]
    applied_ref[...] = applied
    coef = lax.dot_general(
        vectors,
        applied,
        (((0,), (0,)), ((), ())),
        precision=lax.Precision.HIGHEST,
        preferred_element_type=jnp.float32,
    )
    coef_ref[...] = coef
    own_rows = pl.ds(pl.multiple_of(me * rows, rows), rows)
    projection = jnp.dot(
        vectors_ref[own_rows, :],
        coef,
        precision=lax.Precision.HIGHEST,
        preferred_element_type=jnp.float32,
    )
    residual_ref[...] = (applied_ref[own_rows, :] - projection / total).astype(jnp.bfloat16)


def from_peer(value, count, offset):
    return lax.ppermute(value, "blk", [(i, i ^ offset) for i in range(count)])


def shards(frames, basis, density):
    count = lax.axis_size("blk")
    rows, feature_count = frames.shape
    width = basis.shape[1]
    total = rows * count
    whole = pl.BlockSpec(memory_space=pltpu.VMEM)
    params = pltpu.CompilerParams(vmem_limit_bytes=48 << 20)
    features = lax.all_to_all(frames, "blk", split_axis=1, concat_axis=0, tiled=True)
    partial = pl.pallas_call(
        partial_kernel,
        out_shape=jax.ShapeDtypeStruct((total // 2 + 2 * rows, total), jnp.float32),
        in_specs=[whole] + [pl.BlockSpec(memory_space=pltpu.HBM)] * 2,
        out_specs=whole,
        scratch_shapes=[
            pltpu.VMEM(basis.shape, basis.dtype),
            pltpu.VMEM(density.shape, density.dtype),
            pltpu.SemaphoreType.DMA((2,)),
        ],
        compiler_params=params,
    )(
        features,
        pltpu.with_memory_space_constraint(basis, pltpu.HBM),
        pltpu.with_memory_space_constraint(density, pltpu.HBM),
    )
    peers = [from_peer(partial, count, offset) for offset in range(1, PLANE)]
    message = sum(peers, partial).astype(jnp.bfloat16)
    messages = [message] + [
        from_peer(message, count, offset) for offset in range(PLANE, count, PLANE)
    ]
    return pl.pallas_call(
        functools.partial(finish_kernel, feature_count, width, rows),
        out_shape=(
            jax.ShapeDtypeStruct((rows, width), jnp.bfloat16),
            jax.ShapeDtypeStruct((width, width), jnp.float32),
        ),
        in_specs=[whole] * len(messages),
        out_specs=(whole, whole),
        scratch_shapes=[pltpu.VMEM((total, width), jnp.float32)] * 2,
        compiler_params=params,
    )(*messages)


def solution(mesh):
    placed = (P(("groups", "blk"), None), P(("groups", "blk"), None), P(("groups", "blk")))
    return jax.shard_map(
        shards,
        mesh=mesh,
        in_specs=placed,
        out_specs=(P(("groups", "blk"), None), P("groups", None)),
        check_vma=False,
    )
```

time: 32.3 us -> 31.6 us (0.978)
  blocking collectives: 27.7 us -> 17.4 us
  starting transfers between devices: 0.07 us -> 6.38 us
  waiting for transfers between devices: 1.2 us -> 4.73 us
  local copies, waits for them, and re-layouts: 0.68 us -> 0 us
  Pallas kernels: 1.69 us -> 2.09 us
    all_to_all x1 -> x0, blocking collectives: 10.2 us -> none  [shards(): lax.all_to_all(message, 'blk', split_axis=0, concat_axis=0, tiled=True, a...]
    ppermute x1 -> x6, starting transfers between devices: 0.07 us -> 6.38 us  [from_peer(): return lax.ppermute(value, 'blk', [(i, i ^ offset) for i in range(count)])]
    ppermute x1 -> x6, waiting for transfers between devices: 1.2 us -> 4.73 us  [from_peer(): return lax.ppermute(value, 'blk', [(i, i ^ offset) for i in range(count)])]
    unnamed x4 -> x0, local copies, waits for them, and re-layouts: 0.66 us -> none
    pallas_call x1, Pallas kernels: 0.37 us -> 0.78 us  [shards(): pl.pallas_call(partial_kernel, out_shape=jax.ShapeDtypeStruct((total // 2...]
  transfers between devices with their start and end apart: 1 -> 6, of which waited for: 1 -> 5; matrix products, arithmetic and copies ran while one was open for 0% -> 0% of each run, Pallas kernels for 0% -> 0%
where the time goes in v3:
time: 31.6 us; the launch traced here: 31.3 us
  blocking collectives  17.4 us (55%)
  starting transfers between devices  6.38 us (20%)
  waiting for transfers between devices  4.73 us (15%)
  Pallas kernels  2.09 us (7%)
  between operations  0.65 us (2%)
    all_to_all x1, blocking collectives, shards(): lax.all_to_all(frames, 'blk', split_axis=1, concat_axis=0, tiled=True)  17.4 us
    ppermute x6, starting transfers between devices, from_peer(): return lax.ppermute(value, 'blk', [(i, i ^ offset) for i in range(count)])  6.38 us
    ppermute x6, waiting for transfers between devices, from_peer(): return lax.ppermute(value, 'blk', [(i, i ^ offset) for i in range(count)])  4.73 us
    pallas_call x1, Pallas kernels, shards(): pl.pallas_call(functools.partial(finish_kernel, feature_count, width, row...  1.31 us
    pallas_call x1, Pallas kernels, shards(): pl.pallas_call(partial_kernel, out_shape=jax.ShapeDtypeStruct((total // 2...  0.78 us
  transfers between devices with their start and end apart: 6, of which 5 were waited for; matrix products, arithmetic and copies ran while one was open for 0% of the time, Pallas kernels for 0%

profile of v3, /device:TPU:0, one launch (start us, length us, event | category | flops | bytes accessed | tf_op | source)
XLA Modules:
  0.0 31.3 jit_solution(15131072882064860429)
XLA Ops:
  0.6 17.4 %all_to_all.19 = bf16[8,16,1024]{2,0,1:T(8,128)(2,1)S(1)} all-to-all(bf16[8,16,1024]{2,0,1:T(8,128)(2,1)} %bitcast.5), channel_id=1, replica_groups=mesh['groups'=2,'blk'=16] {'blk'}, dimensions={1} | all-to-all | bytes 524288 | tf_op jit(solution)/shard_map/all_to_all | solution.py:120
  18.1 0.8 %shard_map.50 = f32[80,128]{1,0:T(8,128)S(1)} custom-call(bf16[128,1024]{1,0:T(8,128)(2,1)S(1)} %bitcast.4, bf16[8,64]{1,0:T(8,128)(2,1)} %basis_hbm.1, bf16[8]{0:T(256)(128)(2,1)} %density_hbm.1), custom_call_target="tpu_custom_call" | custom-call | tf_op jit(solution)/shard_map/pallas_call | solution.py:121
  18.9 0.2 collective-permute-start.2
  19.1 1.4 %collective-permute-start.1 = (f32[80,128]{1,0:T(8,128)S(1)}, f32[80,128]{1,0:T(8,128)S(1)}, u32[]{:S(2)}, u32[]{:S(2)}) collective-permute-start(f32[80,128]{1,0:T(8,128)S(1)} %shard_map.50), channel_id=1, source_target_pairs={{0,2},{1,3},{2,0},{3,1},{4,6},{5,7},{6,4},{7,5},{8,10},{9,11},{10,... | collective-permute-start | bytes 122888 | tf_op jit(solution)/shard_map/ppermute | solution.py:110
  20.4 0.4 %collective-permute-start = (f32[80,128]{1,0:T(8,128)S(1)}, f32[80,128]{1,0:T(8,128)S(1)}, u32[]{:S(2)}, u32[]{:S(2)}) collective-permute-start(f32[80,128]{1,0:T(8,128)S(1)} %shard_map.50), channel_id=1, source_target_pairs={{0,1},{1,0},{2,3},{3,2},{4,5},{5,4},{6,7},{7,6},{8,9},{9,8},{10,11... | collective-permute-start | bytes 122888 | tf_op jit(solution)/shard_map/ppermute | solution.py:110
  20.8 2.0 %collective-permute-done.2 = f32[80,128]{1,0:T(8,128)S(1)} collective-permute-done((f32[80,128]{1,0:T(8,128)S(1)}, f32[80,128]{1,0:T(8,128)S(1)}, u32[]{:S(2)}, u32[]{:S(2)}) %collective-permute-start.2) | collective-permute-done | bytes 40992 | tf_op jit(solution)/shard_map/ppermute | solution.py:110
  22.8 0.9 %collective-permute-done.1 = f32[80,128]{1,0:T(8,128)S(1)} collective-permute-done((f32[80,128]{1,0:T(8,128)S(1)}, f32[80,128]{1,0:T(8,128)S(1)}, u32[]{:S(2)}, u32[]{:S(2)}) %collective-permute-start.1) | collective-permute-done | bytes 40992 | tf_op jit(solution)/shard_map/ppermute | solution.py:110
  23.7 0.0 collective-permute-done
  23.7 1.3 %collective-permute-start.5 = (bf16[80,128]{1,0:T(8,128)(2,1)S(1)}, bf16[80,128]{1,0:T(8,128)(2,1)S(1)}, u32[]{:S(2)}, u32[]{:S(2)}) collective-permute-start(bf16[80,128]{1,0:T(8,128)(2,1)S(1)} %add_convert_fusion.refs_0_), channel_id=1, source_target_pairs={{0,12},{1,13},{2,14},{3,15},{4,8},{5,9},{6,10},{7,11},{8,4},{9,5},... | collective-permute-start | bytes 61448 | tf_op jit(solution)/shard_map/ppermute | solution.py:110
  25.0 0.7 %collective-permute-start.4 = (bf16[80,128]{1,0:T(8,128)(2,1)S(1)}, bf16[80,128]{1,0:T(8,128)(2,1)S(1)}, u32[]{:S(2)}, u32[]{:S(2)}) collective-permute-start(bf16[80,128]{1,0:T(8,128)(2,1)S(1)} %add_convert_fusion.refs_0_), channel_id=1, source_target_pairs={{0,8},{1,9},{2,10},{3,11},{4,12},{5,13},{6,14},{7,15},{8,0},{9,1},... | collective-permute-start | bytes 61448 | tf_op jit(solution)/shard_map/ppermute | solution.py:110
  25.6 2.5 %collective-permute-start.3 = (bf16[80,128]{1,0:T(8,128)(2,1)S(1)}, bf16[80,128]{1,0:T(8,128)(2,1)S(1)}, u32[]{:S(2)}, u32[]{:S(2)}) collective-permute-start(bf16[80,128]{1,0:T(8,128)(2,1)S(1)} %add_convert_fusion.refs_0_), channel_id=1, source_target_pairs={{0,4},{1,5},{2,6},{3,7},{4,0},{5,1},{6,2},{7,3},{8,12},{9,13},{10,... | collective-permute-start | bytes 61448 | tf_op jit(solution)/shard_map/ppermute | solution.py:110
  28.1 1.2 %collective-permute-done.5.refs_3_ = bf16[80,128]{1,0:T(8,128)(2,1)S(1)} collective-permute-done((bf16[80,128]{1,0:T(8,128)(2,1)S(1)}, bf16[80,128]{1,0:T(8,128)(2,1)S(1)}, u32[]{:S(2)}, u32[]{:S(2)}) %collective-permute-start.5) | collective-permute-done | bytes 20512 | tf_op jit(solution)/shard_map/ppermute | solution.py:110
  29.3 0.4 %collective-permute-done.4.refs_2_ = bf16[80,128]{1,0:T(8,128)(2,1)S(1)} collective-permute-done((bf16[80,128]{1,0:T(8,128)(2,1)S(1)}, bf16[80,128]{1,0:T(8,128)(2,1)S(1)}, u32[]{:S(2)}, u32[]{:S(2)}) %collective-permute-start.4) | collective-permute-done | bytes 20512 | tf_op jit(solution)/shard_map/ppermute | solution.py:110
  29.8 0.2 collective-permute-done.3.refs_1_
  30.0 1.3 %shard_map.51 = (bf16[8,64]{1,0:T(8,128)(2,1)}, f32[64,64]{1,0:T(8,128)}) custom-call(bf16[80,128]{1,0:T(8,128)(2,1)S(1)} %add_convert_fusion.refs_0_, bf16[80,128]{1,0:T(8,128)(2,1)S(1)} %collective-permute-done.3.refs_1_, bf16[80,128]{1,0:T(8,128)(2,1)S(1)} %collective-permute-done.4.refs_2_, bf16[80,128]{1,0:T(8,128)(2,1)S(1)} %collective-permute-done.5.refs_3_), custom_call_target="tpu_custom_call" | custom-call | tf_op jit(solution)/shard_map/pallas_call | solution.py:142
  (1 shorter events, 0.0 us)
Async XLA Ops:
  18.9 3.9 %collective-permute-start.2 = (f32[80,128]{1,0:T(8,128)S(1)}, f32[80,128]{1,0:T(8,128)S(1)}, u32[]{:S(2)}, u32[]{:S(2)}) collective-permute-start(f32[80,128]{1,0:T(8,128)S(1)} %shard_map.50), channel_id=1, source_target_pairs={{0,3},{1,2},{2,1},{3,0},{4,7},{5,6},{6,5},{7,4},{8,11},{9,10},{10,... | collective-permute-start | bytes 122888 | tf_op jit(solution)/shard_map/ppermute | solution.py:110
  19.1 4.6 %collective-permute-start.1 = (f32[80,128]{1,0:T(8,128)S(1)}, f32[80,128]{1,0:T(8,128)S(1)}, u32[]{:S(2)}, u32[]{:S(2)}) collective-permute-start(f32[80,128]{1,0:T(8,128)S(1)} %shard_map.50), channel_id=1, source_target_pairs={{0,2},{1,3},{2,0},{3,1},{4,6},{5,7},{6,4},{7,5},{8,10},{9,11},{10,... | collective-permute-start | bytes 122888 | tf_op jit(solution)/shard_map/ppermute | solution.py:110
  20.4 3.3 %collective-permute-start = (f32[80,128]{1,0:T(8,128)S(1)}, f32[80,128]{1,0:T(8,128)S(1)}, u32[]{:S(2)}, u32[]{:S(2)}) collective-permute-start(f32[80,128]{1,0:T(8,128)S(1)} %shard_map.50), channel_id=1, source_target_pairs={{0,1},{1,0},{2,3},{3,2},{4,5},{5,4},{6,7},{7,6},{8,9},{9,8},{10,11... | collective-permute-start | bytes 122888 | tf_op jit(solution)/shard_map/ppermute | solution.py:110
  23.7 5.6 %collective-permute-start.5 = (bf16[80,128]{1,0:T(8,128)(2,1)S(1)}, bf16[80,128]{1,0:T(8,128)(2,1)S(1)}, u32[]{:S(2)}, u32[]{:S(2)}) collective-permute-start(bf16[80,128]{1,0:T(8,128)(2,1)S(1)} %add_convert_fusion.refs_0_), channel_id=1, source_target_pairs={{0,12},{1,13},{2,14},{3,15},{4,8},{5,9},{6,10},{7,11},{8,4},{9,5},... | collective-permute-start | bytes 61448 | tf_op jit(solution)/shard_map/ppermute | solution.py:110
  25.0 4.8 %collective-permute-start.4 = (bf16[80,128]{1,0:T(8,128)(2,1)S(1)}, bf16[80,128]{1,0:T(8,128)(2,1)S(1)}, u32[]{:S(2)}, u32[]{:S(2)}) collective-permute-start(bf16[80,128]{1,0:T(8,128)(2,1)S(1)} %add_convert_fusion.refs_0_), channel_id=1, source_target_pairs={{0,8},{1,9},{2,10},{3,11},{4,12},{5,13},{6,14},{7,15},{8,0},{9,1},... | collective-permute-start | bytes 61448 | tf_op jit(solution)/shard_map/ppermute | solution.py:110
  25.6 4.3 %collective-permute-start.3 = (bf16[80,128]{1,0:T(8,128)(2,1)S(1)}, bf16[80,128]{1,0:T(8,128)(2,1)S(1)}, u32[]{:S(2)}, u32[]{:S(2)}) collective-permute-start(bf16[80,128]{1,0:T(8,128)(2,1)S(1)} %add_convert_fusion.refs_0_), channel_id=1, source_target_pairs={{0,4},{1,5},{2,6},{3,7},{4,0},{5,1},{6,2},{7,3},{8,12},{9,13},{10,... | collective-permute-start | bytes 61448 | tf_op jit(solution)/shard_map/ppermute | solution.py:110

commit v4 on v3

--- a/solution.py
+++ b/solution.py
@@ -7,7 +7,7 @@
 from jax.experimental.pallas import tpu as pltpu
 from jax.sharding import PartitionSpec as P
 
-PLANE = 4
+CORES = 2
 
 
 def partial_kernel(features_ref, basis_hbm, density_hbm, message_ref, basis_ref, density_ref, sems):
@@ -43,43 +43,52 @@
     density = jnp.concatenate([density, jnp.zeros((1, total - rows), jnp.float32)], axis=1)
     density = pltpu.roll(density, lax.rem(me * rows, half), 1)
     message_ref[:half] = jnp.where(own_row == own_lane, density, packed)
-    place = lax.rem(me, PLANE)
     vectors = jnp.concatenate(
         [basis_ref[...].astype(jnp.float32), jnp.zeros((rows, total - width), jnp.float32)], axis=1
     )
-    vectors = pltpu.roll(vectors, lax.rem(place, 2) * width, 1)
-    message_ref[half : half + rows] = jnp.where(place < 2, vectors, 0.0)
-    message_ref[half + rows :] = jnp.where(place < 2, 0.0, vectors)
+    message_ref[half:] = pltpu.roll(vectors, lax.rem(me, CORES) * width, 1)
+
+
+def routes(pairs):
+    evens = [offset for offset in range(pairs) if offset.bit_count() % 2 == 0]
+    return [(offset, offset ^ (1 if offset < pairs // 2 else 2)) for offset in evens]
 
 
 def finish_kernel(feature_count, width, rows, *refs):
-    planes = len(refs) - 4
-    message_refs = refs[:planes]
-    residual_ref, coef_ref, applied_ref, vectors_ref = refs[planes:]
-    total = message_refs[0].shape[1]
-    half = total // 2
+    residual_ref, coef_ref, applied_ref, vectors_ref = refs[-4:]
+    own_ref, *message_refs = refs[:-4]
+    half = own_ref.shape[1] // 2
+    total = 2 * half
+    pairs = total // (CORES * rows)
     me = lax.axis_index("blk")
-    plane = lax.div(me, PLANE)
-    near = sum(ref[:half].astype(jnp.float32) for ref in message_refs[: planes // 2])
-    far = sum(ref[:half].astype(jnp.float32) for ref in message_refs[planes // 2 :])
+    core, pair = lax.rem(me, CORES), lax.div(me, CORES)
+    steps = routes(pairs)
+    steps = steps + [(two, one) for one, two in steps]
+    near = own_ref[:half].astype(jnp.float32)
+    far = jnp.zeros_like(near)
+    for step, ref in zip(steps, message_refs):
+        if max(step) < pairs // 2:
+            near += ref[:half].astype(jnp.float32)
+        else:
+            far += ref[:half].astype(jnp.float32)
     packed = near + far
     row = lax.broadcasted_iota(jnp.int32, (half, total), 0)
     lane = lax.broadcasted_iota(jnp.int32, (half, total), 1)
     slots = [
         jnp.sum(jnp.where(row == lane, part, 0.0), axis=0, keepdims=True) for part in (near, far)
     ]
-    upper = lax.div(plane, planes // 2)
+    upper = lax.div(pair, pairs // 2)
     density = pltpu.roll(slots[0], upper * half, 1) + pltpu.roll(slots[1], (1 - upper) * half, 1)
     top = jnp.where((lane >= half) | (row < lane), packed, 0.0)
     bottom = pltpu.roll(jnp.where((lane < half) & (row > lane), packed, 0.0), half, 1)
     one_side = jnp.concatenate([top, bottom], axis=0)
     dist = one_side + one_side.T
     weight = (jnp.exp(-dist / feature_count) * density).astype(jnp.bfloat16)
-    for offset, ref in enumerate(message_refs):
-        tail = ref[half:].astype(jnp.float32)
-        base = (plane ^ offset) * PLANE * rows
-        for place in range(PLANE):
-            block = tail[place // 2 * rows :][:rows, place % 2 * width :][:, :width]
+    for step, ref in zip(steps + [(0, 0)], message_refs + [own_ref]):
+        both = ref[half:].astype(jnp.float32)
+        base = (pair ^ jnp.where(core == 0, step[0], step[1])) * CORES * rows
+        for place in range(CORES):
+            block = both[:, place * width : (place + 1) * width]
             vectors_ref[pl.ds(pl.multiple_of(base + place * rows, rows), rows), :] = block
     vectors = vectors_ref[...]
     extended = jnp.concatenate(
@@ -106,8 +115,9 @@
     residual_ref[...] = (applied_ref[own_rows, :] - projection / total).astype(jnp.bfloat16)
 
 
-def from_peer(value, count, offset):
-    return lax.ppermute(value, "blk", [(i, i ^ offset) for i in range(count)])
+def from_peer(value, count, offsets):
+    links = [(i, i ^ offsets[i % CORES]) for i in range(count) if offsets[i % CORES]]
+    return lax.ppermute(value, "blk", links)
 
 
 def shards(frames, basis, density):
@@ -120,7 +130,7 @@
     features = lax.all_to_all(frames, "blk", split_axis=1, concat_axis=0, tiled=True)
     partial = pl.pallas_call(
         partial_kernel,
-        out_shape=jax.ShapeDtypeStruct((total // 2 + 2 * rows, total), jnp.float32),
+        out_shape=jax.ShapeDtypeStruct((total // 2 + rows, total), jnp.float32),
         in_specs=[whole] + [pl.BlockSpec(memory_space=pltpu.HBM)] * 2,
         out_specs=whole,
         scratch_shapes=[
@@ -134,11 +144,13 @@
         pltpu.with_memory_space_constraint(basis, pltpu.HBM),
         pltpu.with_memory_space_constraint(density, pltpu.HBM),
     )
-    peers = [from_peer(partial, count, offset) for offset in range(1, PLANE)]
-    message = sum(peers, partial).astype(jnp.bfloat16)
-    messages = [message] + [
-        from_peer(message, count, offset) for offset in range(PLANE, count, PLANE)
+    sibling = (1, 1)
+    message = (partial + from_peer(partial, count, sibling)).astype(jnp.bfloat16)
+    received = [
+        from_peer(message, count, (CORES * first, CORES * second))
+        for first, second in routes(count // CORES)
     ]
+    messages = [message] + received + [from_peer(part, count, sibling) for part in received]
     return pl.pallas_call(
         functools.partial(finish_kernel, feature_count, width, rows),
         out_shape=(

time: 31.6 us -> 30.3 us (0.959)
  waiting for transfers between devices: 4.73 us -> 3.1 us
    ppermute x6 -> x9, waiting for transfers between devices: 4.73 us -> 3.1 us  [from_peer(): return lax.ppermute(value, 'blk', links)]
    ppermute x6 -> x9, starting transfers between devices: 6.38 us -> 6.66 us  [from_peer(): return lax.ppermute(value, 'blk', links)]
  transfers between devices with their start and end apart: 6 -> 9, of which waited for: 5 -> 6; matrix products, arithmetic and copies ran while one was open for 0% -> 0% of each run, Pallas kernels for 0% -> 0%
where the time goes in v4:
time: 30.3 us; the launch traced here: 30 us
  blocking collectives  17.4 us (57%)
  starting transfers between devices  6.66 us (22%)
  waiting for transfers between devices  3.1 us (10%)
  Pallas kernels  2.09 us (7%)
  between operations  0.68 us (2%)
    all_to_all x1, blocking collectives, shards(): lax.all_to_all(frames, 'blk', split_axis=1, concat_axis=0, tiled=True)  17.4 us
    ppermute x9, starting transfers between devices, from_peer(): return lax.ppermute(value, 'blk', links)  6.66 us
    ppermute x9, waiting for transfers between devices, from_peer(): return lax.ppermute(value, 'blk', links)  3.1 us
    pallas_call x1, Pallas kernels, shards(): pl.pallas_call(functools.partial(finish_kernel, feature_count, width, row...  1.31 us
    pallas_call x1, Pallas kernels, shards(): pl.pallas_call(partial_kernel, out_shape=jax.ShapeDtypeStruct((total // 2...  0.78 us
  transfers between devices with their start and end apart: 9, of which 6 were waited for; matrix products, arithmetic and copies ran while one was open for 0% of the time, Pallas kernels for 0%

profile of v4, /device:TPU:0, one launch (start us, length us, event | category | flops | bytes accessed | tf_op | source)
XLA Modules:
  0.0 30.0 jit_solution(15756301502611042773)
XLA Ops:
  0.6 17.4 %all_to_all.19 = bf16[8,16,1024]{2,0,1:T(8,128)(2,1)S(1)} all-to-all(bf16[8,16,1024]{2,0,1:T(8,128)(2,1)} %bitcast.5), channel_id=1, replica_groups=mesh['groups'=2,'blk'=16] {'blk'}, dimensions={1} | all-to-all | bytes 524288 | tf_op jit(solution)/shard_map/all_to_all | solution.py:130
  18.1 0.8 %shard_map.50 = f32[72,128]{1,0:T(8,128)S(1)} custom-call(bf16[128,1024]{1,0:T(8,128)(2,1)S(1)} %bitcast.4, bf16[8,64]{1,0:T(8,128)(2,1)} %basis_hbm.1, bf16[8]{0:T(256)(128)(2,1)} %density_hbm.1), custom_call_target="tpu_custom_call" | custom-call | tf_op jit(solution)/shard_map/pallas_call | solution.py:131
  18.9 0.1 collective-permute-start
  18.9 1.2 %collective-permute-done = f32[72,128]{1,0:T(8,128)S(1)} collective-permute-done((f32[72,128]{1,0:T(8,128)S(1)}, f32[72,128]{1,0:T(8,128)S(1)}, u32[]{:S(2)}, u32[]{:S(2)}) %collective-permute-start) | collective-permute-done | bytes 36896 | tf_op jit(solution)/shard_map/ppermute | solution.py:120
  20.1 1.1 %collective-permute-start.4 = (bf16[72,128]{1,0:T(8,128)(2,1)S(1)}, bf16[72,128]{1,0:T(8,128)(2,1)S(1)}, u32[]{:S(2)}, u32[]{:S(2)}) collective-permute-start(bf16[72,128]{1,0:T(8,128)(2,1)S(1)} %add_convert_fusion.refs_0_), channel_id=1, source_target_pairs={{0,12},{1,9},{2,14},{3,11},{4,8},{5,13},{6,10},{7,15},{8,4},{9,1},... | collective-permute-start | bytes 55304 | tf_op jit(solution)/shard_map/ppermute | solution.py:120
  21.2 1.1 %collective-permute-start.3 = (bf16[72,128]{1,0:T(8,128)(2,1)S(1)}, bf16[72,128]{1,0:T(8,128)(2,1)S(1)}, u32[]{:S(2)}, u32[]{:S(2)}) collective-permute-start(bf16[72,128]{1,0:T(8,128)(2,1)S(1)} %add_convert_fusion.refs_0_), channel_id=1, source_target_pairs={{0,10},{1,15},{2,8},{3,13},{4,14},{5,11},{6,12},{7,9},{8,2},{9,7},... | collective-permute-start | bytes 55304 | tf_op jit(solution)/shard_map/ppermute | solution.py:120
  22.3 3.2 %collective-permute-start.2 = (bf16[72,128]{1,0:T(8,128)(2,1)S(1)}, bf16[72,128]{1,0:T(8,128)(2,1)S(1)}, u32[]{:S(2)}, u32[]{:S(2)}) collective-permute-start(bf16[72,128]{1,0:T(8,128)(2,1)S(1)} %add_convert_fusion.refs_0_), channel_id=1, source_target_pairs={{0,6},{1,5},{2,4},{3,7},{4,2},{5,1},{6,0},{7,3},{8,14},{9,13},{10,... | collective-permute-start | bytes 55304 | tf_op jit(solution)/shard_map/ppermute | solution.py:120
  25.5 0.7 %collective-permute-start.1 = (bf16[72,128]{1,0:T(8,128)(2,1)S(1)}, bf16[72,128]{1,0:T(8,128)(2,1)S(1)}, u32[]{:S(2)}, u32[]{:S(2)}) collective-permute-start(bf16[72,128]{1,0:T(8,128)(2,1)S(1)} %add_convert_fusion.refs_0_), channel_id=1, source_target_pairs={{1,3},{3,1},{5,7},{7,5},{9,11},{11,9},{13,15},{15,13},{17,19},{19,... | collective-permute-start | bytes 55304 | tf_op jit(solution)/shard_map/ppermute | solution.py:120
  26.2 0.0 collective-permute-done.4.refs_4_
  26.2 0.1 collective-permute-start.8
  26.2 0.7 %collective-permute-done.3.refs_3_ = bf16[72,128]{1,0:T(8,128)(2,1)S(1)} collective-permute-done((bf16[72,128]{1,0:T(8,128)(2,1)S(1)}, bf16[72,128]{1,0:T(8,128)(2,1)S(1)}, u32[]{:S(2)}, u32[]{:S(2)}) %collective-permute-start.3) | collective-permute-done | bytes 18464 | tf_op jit(solution)/shard_map/ppermute | solution.py:120
  27.0 0.0 collective-permute-start.7
  27.0 0.3 collective-permute-done.2.refs_2_
  27.2 0.2 collective-permute-start.6
  27.5 0.0 collective-permute-done.1.refs_1_
  27.5 0.3 collective-permute-start.5
  27.8 0.0 collective-permute-done.8.refs_8_
  27.8 0.4 %collective-permute-done.7.refs_7_ = bf16[72,128]{1,0:T(8,128)(2,1)S(1)} collective-permute-done((bf16[72,128]{1,0:T(8,128)(2,1)S(1)}, bf16[72,128]{1,0:T(8,128)(2,1)S(1)}, u32[]{:S(2)}, u32[]{:S(2)}) %collective-permute-start.7) | collective-permute-done | bytes 18464 | tf_op jit(solution)/shard_map/ppermute | solution.py:120
  28.1 0.3 collective-permute-done.6.refs_6_
  28.4 0.2 collective-permute-done.5.refs_5_
  28.7 1.3 %shard_map.51 = (bf16[8,64]{1,0:T(8,128)(2,1)}, f32[64,64]{1,0:T(8,128)}) custom-call(bf16[72,128]{1,0:T(8,128)(2,1)S(1)} %add_convert_fusion.refs_0_, bf16[72,128]{1,0:T(8,128)(2,1)S(1)} %collective-permute-done.1.refs_1_, bf16[72,128]{1,0:T(8,128)(2,1)S(1)} %collective-permute-done.2.refs_2_, bf16[72,128]{1,0:T(8,128)(2,1)S(1)} %collective-permute-done.3.refs_3_, ...), custom_call_target="tpu_custom_call" | custom-call | tf_op jit(solution)/shard_map/pallas_call | solution.py:154
  (1 shorter events, 0.0 us)
Async XLA Ops:
  18.9 1.3 %collective-permute-start = (f32[72,128]{1,0:T(8,128)S(1)}, f32[72,128]{1,0:T(8,128)S(1)}, u32[]{:S(2)}, u32[]{:S(2)}) collective-permute-start(f32[72,128]{1,0:T(8,128)S(1)} %shard_map.50), channel_id=1, source_target_pairs={{0,1},{1,0},{2,3},{3,2},{4,5},{5,4},{6,7},{7,6},{8,9},{9,8},{10,11... | collective-permute-start | bytes 110600 | tf_op jit(solution)/shard_map/ppermute | solution.py:120
  20.1 6.0 %collective-permute-start.4 = (bf16[72,128]{1,0:T(8,128)(2,1)S(1)}, bf16[72,128]{1,0:T(8,128)(2,1)S(1)}, u32[]{:S(2)}, u32[]{:S(2)}) collective-permute-start(bf16[72,128]{1,0:T(8,128)(2,1)S(1)} %add_convert_fusion.refs_0_), channel_id=1, source_target_pairs={{0,12},{1,9},{2,14},{3,11},{4,8},{5,13},{6,10},{7,15},{8,4},{9,1},... | collective-permute-start | bytes 55304 | tf_op jit(solution)/shard_map/ppermute | solution.py:120
  21.2 5.8 %collective-permute-start.3 = (bf16[72,128]{1,0:T(8,128)(2,1)S(1)}, bf16[72,128]{1,0:T(8,128)(2,1)S(1)}, u32[]{:S(2)}, u32[]{:S(2)}) collective-permute-start(bf16[72,128]{1,0:T(8,128)(2,1)S(1)} %add_convert_fusion.refs_0_), channel_id=1, source_target_pairs={{0,10},{1,15},{2,8},{3,13},{4,14},{5,11},{6,12},{7,9},{8,2},{9,7},... | collective-permute-start | bytes 55304 | tf_op jit(solution)/shard_map/ppermute | solution.py:120
  22.3 5.0 %collective-permute-start.2 = (bf16[72,128]{1,0:T(8,128)(2,1)S(1)}, bf16[72,128]{1,0:T(8,128)(2,1)S(1)}, u32[]{:S(2)}, u32[]{:S(2)}) collective-permute-start(bf16[72,128]{1,0:T(8,128)(2,1)S(1)} %add_convert_fusion.refs_0_), channel_id=1, source_target_pairs={{0,6},{1,5},{2,4},{3,7},{4,2},{5,1},{6,0},{7,3},{8,14},{9,13},{10,... | collective-permute-start | bytes 55304 | tf_op jit(solution)/shard_map/ppermute | solution.py:120
  25.5 2.0 %collective-permute-start.1 = (bf16[72,128]{1,0:T(8,128)(2,1)S(1)}, bf16[72,128]{1,0:T(8,128)(2,1)S(1)}, u32[]{:S(2)}, u32[]{:S(2)}) collective-permute-start(bf16[72,128]{1,0:T(8,128)(2,1)S(1)} %add_convert_fusion.refs_0_), channel_id=1, source_target_pairs={{1,3},{3,1},{5,7},{7,5},{9,11},{11,9},{13,15},{15,13},{17,19},{19,... | collective-permute-start | bytes 55304 | tf_op jit(solution)/shard_map/ppermute | solution.py:120
  26.2 1.6 %collective-permute-start.8 = (bf16[72,128]{1,0:T(8,128)(2,1)S(1)}, bf16[72,128]{1,0:T(8,128)(2,1)S(1)}, u32[]{:S(2)}, u32[]{:S(2)}) collective-permute-start(bf16[72,128]{1,0:T(8,128)(2,1)S(1)} %collective-permute-done.4.refs_4_), channel_id=1, source_target_pairs={{0,1},{1,0},{2,3},{3,2},{4,5},{5,4},{6,7},{7,6},{8,9},{9,8},{10,11... | collective-permute-start | bytes 55304 | tf_op jit(solution)/shard_map/ppermute | solution.py:120
  27.0 1.2 %collective-permute-start.7 = (bf16[72,128]{1,0:T(8,128)(2,1)S(1)}, bf16[72,128]{1,0:T(8,128)(2,1)S(1)}, u32[]{:S(2)}, u32[]{:S(2)}) collective-permute-start(bf16[72,128]{1,0:T(8,128)(2,1)S(1)} %collective-permute-done.3.refs_3_), channel_id=1, source_target_pairs={{0,1},{1,0},{2,3},{3,2},{4,5},{5,4},{6,7},{7,6},{8,9},{9,8},{10,11... | collective-permute-start | bytes 55304 | tf_op jit(solution)/shard_map/ppermute | solution.py:120
  27.2 1.2 %collective-permute-start.6 = (bf16[72,128]{1,0:T(8,128)(2,1)S(1)}, bf16[72,128]{1,0:T(8,128)(2,1)S(1)}, u32[]{:S(2)}, u32[]{:S(2)}) collective-permute-start(bf16[72,128]{1,0:T(8,128)(2,1)S(1)} %collective-permute-done.2.refs_2_), channel_id=1, source_target_pairs={{0,1},{1,0},{2,3},{3,2},{4,5},{5,4},{6,7},{7,6},{8,9},{9,8},{10,11... | collective-permute-start | bytes 55304 | tf_op jit(solution)/shard_map/ppermute | solution.py:120
  27.5 1.2 %collective-permute-start.5 = (bf16[72,128]{1,0:T(8,128)(2,1)S(1)}, bf16[72,128]{1,0:T(8,128)(2,1)S(1)}, u32[]{:S(2)}, u32[]{:S(2)}) collective-permute-start(bf16[72,128]{1,0:T(8,128)(2,1)S(1)} %collective-permute-done.1.refs_1_), channel_id=1, source_target_pairs={{0,1},{1,0},{2,3},{3,2},{4,5},{5,4},{6,7},{7,6},{8,9},{9,8},{10,11... | collective-permute-start | bytes 55304 | tf_op jit(solution)/shard_map/ppermute | solution.py:120

commit v5 on v4

--- a/solution.py
+++ b/solution.py
@@ -54,6 +54,12 @@
     return [(offset, offset ^ (1 if offset < pairs // 2 else 2)) for offset in evens]
 
 
+def pieces(value):
+    high = value.astype(jnp.bfloat16).astype(jnp.float32)
+    middle = (value - high).astype(jnp.bfloat16).astype(jnp.float32)
+    return high, middle, (value - high - middle).astype(jnp.bfloat16).astype(jnp.float32)
+
+
 def finish_kernel(feature_count, width, rows, *refs):
     residual_ref, coef_ref, applied_ref, vectors_ref = refs[-4:]
     own_ref, *message_refs = refs[:-4]
@@ -91,27 +97,26 @@
             block = both[:, place * width : (place + 1) * width]
             vectors_ref[pl.ds(pl.multiple_of(base + place * rows, rows), rows), :] = block
     vectors = vectors_ref[...]
+    own_rows = pl.ds(pl.multiple_of(me * rows, rows), rows)
     extended = jnp.concatenate(
         [vectors, jnp.ones((total, 1), jnp.float32), jnp.zeros((total, width - 1), jnp.float32)], axis=1
     )
+    overlaps = lax.dot_general(
+        vectors_ref[own_rows, :].astype(jnp.bfloat16),
+        vectors.astype(jnp.bfloat16),
+        (((1,), (1,)), ((), ())),
+        preferred_element_type=jnp.float32,
+    )
+    left = jnp.concatenate([vectors.T, *pieces(overlaps)], axis=0).astype(jnp.bfloat16)
     numer = jnp.dot(weight, extended.astype(jnp.bfloat16), preferred_element_type=jnp.float32)
     applied = numer[:, :width] / numer[:, width : width + 1]
     applied_ref[...] = applied
-    coef = lax.dot_general(
-        vectors,
-        applied,
-        (((0,), (0,)), ((), ())),
-        precision=lax.Precision.HIGHEST,
-        preferred_element_type=jnp.float32,
+    product = sum(
+        jnp.dot(left, piece.astype(jnp.bfloat16), preferred_element_type=jnp.float32)
+        for piece in reversed(pieces(applied))
     )
-    coef_ref[...] = coef
-    own_rows = pl.ds(pl.multiple_of(me * rows, rows), rows)
-    projection = jnp.dot(
-        vectors_ref[own_rows, :],
-        coef,
-        precision=lax.Precision.HIGHEST,
-        preferred_element_type=jnp.float32,
-    )
+    coef_ref[...] = product[:width]
+    projection = sum(product[width + part * rows :][:rows] for part in reversed(range(3)))
     residual_ref[...] = (applied_ref[own_rows, :] - projection / total).astype(jnp.bfloat16)
 
 

time: 30.3 us -> 30.1 us (level)
  no operation moved by 1% of the time
where the time goes in v5:
time: 30.1 us; the launch traced here: 29.8 us
  blocking collectives  17.4 us (58%)
  starting transfers between devices  6.66 us (22%)
  waiting for transfers between devices  3.1 us (10%)
  Pallas kernels  1.93 us (6%)
  between operations  0.68 us (2%)
    all_to_all x1, blocking collectives, shards(): lax.all_to_all(frames, 'blk', split_axis=1, concat_axis=0, tiled=True)  17.4 us
    ppermute x9, starting transfers between devices, from_peer(): return lax.ppermute(value, 'blk', links)  6.66 us
    ppermute x9, waiting for transfers between devices, from_peer(): return lax.ppermute(value, 'blk', links)  3.1 us
    pallas_call x1, Pallas kernels, shards(): pl.pallas_call(functools.partial(finish_kernel, feature_count, width, row...  1.15 us
    pallas_call x1, Pallas kernels, shards(): pl.pallas_call(partial_kernel, out_shape=jax.ShapeDtypeStruct((total // 2...  0.78 us
  transfers between devices with their start and end apart: 9, of which 6 were waited for; matrix products, arithmetic and copies ran while one was open for 0% of the time, Pallas kernels for 0%

profile of v5, /device:TPU:0, one launch (start us, length us, event | category | flops | bytes accessed | tf_op | source)
XLA Modules:
  0.0 29.8 jit_solution(14801400558719920485)
XLA Ops:
  0.6 17.4 %all_to_all.19 = bf16[8,16,1024]{2,0,1:T(8,128)(2,1)S(1)} all-to-all(bf16[8,16,1024]{2,0,1:T(8,128)(2,1)} %bitcast.5), channel_id=1, replica_groups=mesh['groups'=2,'blk'=16] {'blk'}, dimensions={1} | all-to-all | bytes 524288 | tf_op jit(solution)/shard_map/all_to_all | solution.py:135
  18.1 0.8 %shard_map.50 = f32[72,128]{1,0:T(8,128)S(1)} custom-call(bf16[128,1024]{1,0:T(8,128)(2,1)S(1)} %bitcast.4, bf16[8,64]{1,0:T(8,128)(2,1)} %basis_hbm.1, bf16[8]{0:T(256)(128)(2,1)} %density_hbm.1), custom_call_target="tpu_custom_call" | custom-call | tf_op jit(solution)/shard_map/pallas_call | solution.py:136
  18.9 0.1 collective-permute-start
  18.9 1.2 %collective-permute-done = f32[72,128]{1,0:T(8,128)S(1)} collective-permute-done((f32[72,128]{1,0:T(8,128)S(1)}, f32[72,128]{1,0:T(8,128)S(1)}, u32[]{:S(2)}, u32[]{:S(2)}) %collective-permute-start) | collective-permute-done | bytes 36896 | tf_op jit(solution)/shard_map/ppermute | solution.py:125
  20.1 1.1 %collective-permute-start.4 = (bf16[72,128]{1,0:T(8,128)(2,1)S(1)}, bf16[72,128]{1,0:T(8,128)(2,1)S(1)}, u32[]{:S(2)}, u32[]{:S(2)}) collective-permute-start(bf16[72,128]{1,0:T(8,128)(2,1)S(1)} %add_convert_fusion.refs_0_), channel_id=1, source_target_pairs={{0,12},{1,9},{2,14},{3,11},{4,8},{5,13},{6,10},{7,15},{8,4},{9,1},... | collective-permute-start | bytes 55304 | tf_op jit(solution)/shard_map/ppermute | solution.py:125
  21.2 1.1 %collective-permute-start.3 = (bf16[72,128]{1,0:T(8,128)(2,1)S(1)}, bf16[72,128]{1,0:T(8,128)(2,1)S(1)}, u32[]{:S(2)}, u32[]{:S(2)}) collective-permute-start(bf16[72,128]{1,0:T(8,128)(2,1)S(1)} %add_convert_fusion.refs_0_), channel_id=1, source_target_pairs={{0,10},{1,15},{2,8},{3,13},{4,14},{5,11},{6,12},{7,9},{8,2},{9,7},... | collective-permute-start | bytes 55304 | tf_op jit(solution)/shard_map/ppermute | solution.py:125
  22.3 3.2 %collective-permute-start.2 = (bf16[72,128]{1,0:T(8,128)(2,1)S(1)}, bf16[72,128]{1,0:T(8,128)(2,1)S(1)}, u32[]{:S(2)}, u32[]{:S(2)}) collective-permute-start(bf16[72,128]{1,0:T(8,128)(2,1)S(1)} %add_convert_fusion.refs_0_), channel_id=1, source_target_pairs={{0,6},{1,5},{2,4},{3,7},{4,2},{5,1},{6,0},{7,3},{8,14},{9,13},{10,... | collective-permute-start | bytes 55304 | tf_op jit(solution)/shard_map/ppermute | solution.py:125
  25.5 0.7 %collective-permute-start.1 = (bf16[72,128]{1,0:T(8,128)(2,1)S(1)}, bf16[72,128]{1,0:T(8,128)(2,1)S(1)}, u32[]{:S(2)}, u32[]{:S(2)}) collective-permute-start(bf16[72,128]{1,0:T(8,128)(2,1)S(1)} %add_convert_fusion.refs_0_), channel_id=1, source_target_pairs={{1,3},{3,1},{5,7},{7,5},{9,11},{11,9},{13,15},{15,13},{17,19},{19,... | collective-permute-start | bytes 55304 | tf_op jit(solution)/shard_map/ppermute | solution.py:125
  26.2 0.0 collective-permute-done.4.refs_4_
  26.2 0.1 collective-permute-start.8
  26.2 0.7 %collective-permute-done.3.refs_3_ = bf16[72,128]{1,0:T(8,128)(2,1)S(1)} collective-permute-done((bf16[72,128]{1,0:T(8,128)(2,1)S(1)}, bf16[72,128]{1,0:T(8,128)(2,1)S(1)}, u32[]{:S(2)}, u32[]{:S(2)}) %collective-permute-start.3) | collective-permute-done | bytes 18464 | tf_op jit(solution)/shard_map/ppermute | solution.py:125
  27.0 0.0 collective-permute-start.7
  27.0 0.3 collective-permute-done.2.refs_2_
  27.2 0.2 collective-permute-start.6
  27.5 0.0 collective-permute-done.1.refs_1_
  27.5 0.3 collective-permute-start.5
  27.8 0.0 collective-permute-done.8.refs_8_
  27.8 0.4 %collective-permute-done.7.refs_7_ = bf16[72,128]{1,0:T(8,128)(2,1)S(1)} collective-permute-done((bf16[72,128]{1,0:T(8,128)(2,1)S(1)}, bf16[72,128]{1,0:T(8,128)(2,1)S(1)}, u32[]{:S(2)}, u32[]{:S(2)}) %collective-permute-start.7) | collective-permute-done | bytes 18464 | tf_op jit(solution)/shard_map/ppermute | solution.py:125
  28.1 0.3 collective-permute-done.6.refs_6_
  28.4 0.2 collective-permute-done.5.refs_5_
  28.7 1.1 %shard_map.51 = (bf16[8,64]{1,0:T(8,128)(2,1)}, f32[64,64]{1,0:T(8,128)}) custom-call(bf16[72,128]{1,0:T(8,128)(2,1)S(1)} %add_convert_fusion.refs_0_, bf16[72,128]{1,0:T(8,128)(2,1)S(1)} %collective-permute-done.1.refs_1_, bf16[72,128]{1,0:T(8,128)(2,1)S(1)} %collective-permute-done.2.refs_2_, bf16[72,128]{1,0:T(8,128)(2,1)S(1)} %collective-permute-done.3.refs_3_, ...), custom_call_target="tpu_custom_call" | custom-call | tf_op jit(solution)/shard_map/pallas_call | solution.py:159
  (1 shorter events, 0.0 us)
Async XLA Ops:
  18.9 1.3 %collective-permute-start = (f32[72,128]{1,0:T(8,128)S(1)}, f32[72,128]{1,0:T(8,128)S(1)}, u32[]{:S(2)}, u32[]{:S(2)}) collective-permute-start(f32[72,128]{1,0:T(8,128)S(1)} %shard_map.50), channel_id=1, source_target_pairs={{0,1},{1,0},{2,3},{3,2},{4,5},{5,4},{6,7},{7,6},{8,9},{9,8},{10,11... | collective-permute-start | bytes 110600 | tf_op jit(solution)/shard_map/ppermute | solution.py:125
  20.1 6.0 %collective-permute-start.4 = (bf16[72,128]{1,0:T(8,128)(2,1)S(1)}, bf16[72,128]{1,0:T(8,128)(2,1)S(1)}, u32[]{:S(2)}, u32[]{:S(2)}) collective-permute-start(bf16[72,128]{1,0:T(8,128)(2,1)S(1)} %add_convert_fusion.refs_0_), channel_id=1, source_target_pairs={{0,12},{1,9},{2,14},{3,11},{4,8},{5,13},{6,10},{7,15},{8,4},{9,1},... | collective-permute-start | bytes 55304 | tf_op jit(solution)/shard_map/ppermute | solution.py:125
  21.2 5.8 %collective-permute-start.3 = (bf16[72,128]{1,0:T(8,128)(2,1)S(1)}, bf16[72,128]{1,0:T(8,128)(2,1)S(1)}, u32[]{:S(2)}, u32[]{:S(2)}) collective-permute-start(bf16[72,128]{1,0:T(8,128)(2,1)S(1)} %add_convert_fusion.refs_0_), channel_id=1, source_target_pairs={{0,10},{1,15},{2,8},{3,13},{4,14},{5,11},{6,12},{7,9},{8,2},{9,7},... | collective-permute-start | bytes 55304 | tf_op jit(solution)/shard_map/ppermute | solution.py:125
  22.3 5.0 %collective-permute-start.2 = (bf16[72,128]{1,0:T(8,128)(2,1)S(1)}, bf16[72,128]{1,0:T(8,128)(2,1)S(1)}, u32[]{:S(2)}, u32[]{:S(2)}) collective-permute-start(bf16[72,128]{1,0:T(8,128)(2,1)S(1)} %add_convert_fusion.refs_0_), channel_id=1, source_target_pairs={{0,6},{1,5},{2,4},{3,7},{4,2},{5,1},{6,0},{7,3},{8,14},{9,13},{10,... | collective-permute-start | bytes 55304 | tf_op jit(solution)/shard_map/ppermute | solution.py:125
  25.5 2.0 %collective-permute-start.1 = (bf16[72,128]{1,0:T(8,128)(2,1)S(1)}, bf16[72,128]{1,0:T(8,128)(2,1)S(1)}, u32[]{:S(2)}, u32[]{:S(2)}) collective-permute-start(bf16[72,128]{1,0:T(8,128)(2,1)S(1)} %add_convert_fusion.refs_0_), channel_id=1, source_target_pairs={{1,3},{3,1},{5,7},{7,5},{9,11},{11,9},{13,15},{15,13},{17,19},{19,... | collective-permute-start | bytes 55304 | tf_op jit(solution)/shard_map/ppermute | solution.py:125
  26.2 1.6 %collective-permute-start.8 = (bf16[72,128]{1,0:T(8,128)(2,1)S(1)}, bf16[72,128]{1,0:T(8,128)(2,1)S(1)}, u32[]{:S(2)}, u32[]{:S(2)}) collective-permute-start(bf16[72,128]{1,0:T(8,128)(2,1)S(1)} %collective-permute-done.4.refs_4_), channel_id=1, source_target_pairs={{0,1},{1,0},{2,3},{3,2},{4,5},{5,4},{6,7},{7,6},{8,9},{9,8},{10,11... | collective-permute-start | bytes 55304 | tf_op jit(solution)/shard_map/ppermute | solution.py:125
  27.0 1.2 %collective-permute-start.7 = (bf16[72,128]{1,0:T(8,128)(2,1)S(1)}, bf16[72,128]{1,0:T(8,128)(2,1)S(1)}, u32[]{:S(2)}, u32[]{:S(2)}) collective-permute-start(bf16[72,128]{1,0:T(8,128)(2,1)S(1)} %collective-permute-done.3.refs_3_), channel_id=1, source_target_pairs={{0,1},{1,0},{2,3},{3,2},{4,5},{5,4},{6,7},{7,6},{8,9},{9,8},{10,11... | collective-permute-start | bytes 55304 | tf_op jit(solution)/shard_map/ppermute | solution.py:125
  27.2 1.2 %collective-permute-start.6 = (bf16[72,128]{1,0:T(8,128)(2,1)S(1)}, bf16[72,128]{1,0:T(8,128)(2,1)S(1)}, u32[]{:S(2)}, u32[]{:S(2)}) collective-permute-start(bf16[72,128]{1,0:T(8,128)(2,1)S(1)} %collective-permute-done.2.refs_2_), channel_id=1, source_target_pairs={{0,1},{1,0},{2,3},{3,2},{4,5},{5,4},{6,7},{7,6},{8,9},{9,8},{10,11... | collective-permute-start | bytes 55304 | tf_op jit(solution)/shard_map/ppermute | solution.py:125
  27.5 1.2 %collective-permute-start.5 = (bf16[72,128]{1,0:T(8,128)(2,1)S(1)}, bf16[72,128]{1,0:T(8,128)(2,1)S(1)}, u32[]{:S(2)}, u32[]{:S(2)}) collective-permute-start(bf16[72,128]{1,0:T(8,128)(2,1)S(1)} %collective-permute-done.1.refs_1_), channel_id=1, source_target_pairs={{0,1},{1,0},{2,3},{3,2},{4,5},{5,4},{6,7},{7,6},{8,9},{9,8},{10,11... | collective-permute-start | bytes 55304 | tf_op jit(solution)/shard_map/ppermute | solution.py:125

commit v6 on v5

--- a/solution.py
+++ b/solution.py
@@ -50,8 +50,9 @@
 
 
 def routes(pairs):
-    evens = [offset for offset in range(pairs) if offset.bit_count() % 2 == 0]
-    return [(offset, offset ^ (1 if offset < pairs // 2 else 2)) for offset in evens]
+    half, quarter = pairs // 2, pairs // 4
+    near = [(offset, offset + 1) for offset in range(2, half, 2)]
+    return [(1, 1)] + near + [(half + step, half + quarter + step) for step in range(quarter)]
 
 
 def pieces(value):
@@ -69,7 +70,7 @@
     me = lax.axis_index("blk")
     core, pair = lax.rem(me, CORES), lax.div(me, CORES)
     steps = routes(pairs)
-    steps = steps + [(two, one) for one, two in steps]
+    steps = steps + [(two, one) for one, two in steps[1:]]
     near = own_ref[:half].astype(jnp.float32)
     far = jnp.zeros_like(near)
     for step, ref in zip(steps, message_refs):
@@ -121,8 +122,7 @@
 
 
 def from_peer(value, count, offsets):
-    links = [(i, i ^ offsets[i % CORES]) for i in range(count) if offsets[i % CORES]]
-    return lax.ppermute(value, "blk", links)
+    return lax.ppermute(value, "blk", [(i, i ^ offsets[i % CORES]) for i in range(count)])
 
 
 def shards(frames, basis, density):
@@ -155,7 +155,7 @@
         from_peer(message, count, (CORES * first, CORES * second))
         for first, second in routes(count // CORES)
     ]
-    messages = [message] + received + [from_peer(part, count, sibling) for part in received]
+    messages = [message] + received + [from_peer(part, count, sibling) for part in received[1:]]
     return pl.pallas_call(
         functools.partial(finish_kernel, feature_count, width, rows),
         out_shape=(

time: 30.1 us -> 29.4 us (0.977)
  starting transfers between devices: 6.66 us -> 6 us
    ppermute x9 -> x8, starting transfers between devices: 6.66 us -> 6 us  [from_peer(): lax.ppermute(value, 'blk', [(i, i ^ offsets[i % CORES]) for i in range(co...]
    ppermute x9 -> x8, waiting for transfers between devices: 3.1 us -> 3.11 us  [from_peer(): lax.ppermute(value, 'blk', [(i, i ^ offsets[i % CORES]) for i in range(co...]
  transfers between devices with their start and end apart: 9 -> 8, of which waited for: 6 -> 4; matrix products, arithmetic and copies ran while one was open for 0% -> 0% of each run, Pallas kernels for 0% -> 0%
where the time goes in v6:
time: 29.4 us; the launch traced here: 29.2 us
  blocking collectives  17.4 us (59%)
  starting transfers between devices  6 us (20%)
  waiting for transfers between devices  3.11 us (11%)
  Pallas kernels  1.93 us (7%)
  between operations  0.66 us (2%)
    all_to_all x1, blocking collectives, shards(): lax.all_to_all(frames, 'blk', split_axis=1, concat_axis=0, tiled=True)  17.4 us
    ppermute x8, starting transfers between devices, from_peer(): lax.ppermute(value, 'blk', [(i, i ^ offsets[i % CORES]) for i in range(co...  6 us
    ppermute x8, waiting for transfers between devices, from_peer(): lax.ppermute(value, 'blk', [(i, i ^ offsets[i % CORES]) for i in range(co...  3.11 us
    pallas_call x1, Pallas kernels, shards(): pl.pallas_call(functools.partial(finish_kernel, feature_count, width, row...  1.15 us
    pallas_call x1, Pallas kernels, shards(): pl.pallas_call(partial_kernel, out_shape=jax.ShapeDtypeStruct((total // 2...  0.78 us
  transfers between devices with their start and end apart: 8, of which 4 were waited for; matrix products, arithmetic and copies ran while one was open for 0% of the time, Pallas kernels for 0%

profile of v6, /device:TPU:0, one launch (start us, length us, event | category | flops | bytes accessed | tf_op | source)
XLA Modules:
  0.0 29.2 jit_solution(13907797911999333576)
XLA Ops:
  0.6 17.4 %all_to_all.19 = bf16[8,16,1024]{2,0,1:T(8,128)(2,1)S(1)} all-to-all(bf16[8,16,1024]{2,0,1:T(8,128)(2,1)} %bitcast.5), channel_id=1, replica_groups=mesh['groups'=2,'blk'=16] {'blk'}, dimensions={1} | all-to-all | bytes 524288 | tf_op jit(solution)/shard_map/all_to_all | solution.py:135
  18.1 0.8 %shard_map.50 = f32[72,128]{1,0:T(8,128)S(1)} custom-call(bf16[128,1024]{1,0:T(8,128)(2,1)S(1)} %bitcast.4, bf16[8,64]{1,0:T(8,128)(2,1)} %basis_hbm.1, bf16[8]{0:T(256)(128)(2,1)} %density_hbm.1), custom_call_target="tpu_custom_call" | custom-call | tf_op jit(solution)/shard_map/pallas_call | solution.py:136
  18.9 0.1 collective-permute-start
  18.9 1.2 %collective-permute-done = f32[72,128]{1,0:T(8,128)S(1)} collective-permute-done((f32[72,128]{1,0:T(8,128)S(1)}, f32[72,128]{1,0:T(8,128)S(1)}, u32[]{:S(2)}, u32[]{:S(2)}) %collective-permute-start) | collective-permute-done | bytes 36896 | tf_op jit(solution)/shard_map/ppermute | solution.py:125
  20.1 0.2 collective-permute-start.4
  20.4 2.3 %collective-permute-start.3 = (bf16[72,128]{1,0:T(8,128)(2,1)S(1)}, bf16[72,128]{1,0:T(8,128)(2,1)S(1)}, u32[]{:S(2)}, u32[]{:S(2)}) collective-permute-start(bf16[72,128]{1,0:T(8,128)(2,1)S(1)} %add_convert_fusion.refs_0_), channel_id=1, source_target_pairs={{0,8},{1,13},{2,10},{3,15},{4,12},{5,9},{6,14},{7,11},{8,0},{9,5},... | collective-permute-start | bytes 55304 | tf_op jit(solution)/shard_map/ppermute | solution.py:125
  22.7 1.0 %collective-permute-start.2 = (bf16[72,128]{1,0:T(8,128)(2,1)S(1)}, bf16[72,128]{1,0:T(8,128)(2,1)S(1)}, u32[]{:S(2)}, u32[]{:S(2)}) collective-permute-start(bf16[72,128]{1,0:T(8,128)(2,1)S(1)} %add_convert_fusion.refs_0_), channel_id=1, source_target_pairs={{0,4},{1,7},{2,6},{3,5},{4,0},{5,3},{6,2},{7,1},{8,12},{9,15},{10,... | collective-permute-start | bytes 55304 | tf_op jit(solution)/shard_map/ppermute | solution.py:125
  23.7 1.2 %collective-permute-start.1 = (bf16[72,128]{1,0:T(8,128)(2,1)S(1)}, bf16[72,128]{1,0:T(8,128)(2,1)S(1)}, u32[]{:S(2)}, u32[]{:S(2)}) collective-permute-start(bf16[72,128]{1,0:T(8,128)(2,1)S(1)} %add_convert_fusion.refs_0_), channel_id=1, source_target_pairs={{0,2},{1,3},{2,0},{3,1},{4,6},{5,7},{6,4},{7,5},{8,10},{9,11},{10,... | collective-permute-start | bytes 55304 | tf_op jit(solution)/shard_map/ppermute | solution.py:125
  24.9 1.1 %collective-permute-done.4.refs_4_ = bf16[72,128]{1,0:T(8,128)(2,1)S(1)} collective-permute-done((bf16[72,128]{1,0:T(8,128)(2,1)S(1)}, bf16[72,128]{1,0:T(8,128)(2,1)S(1)}, u32[]{:S(2)}, u32[]{:S(2)}) %collective-permute-start.4) | collective-permute-done | bytes 18464 | tf_op jit(solution)/shard_map/ppermute | solution.py:125
  26.0 0.0 collective-permute-start.7
  26.0 0.0 collective-permute-done.3.refs_3_
  26.0 0.5 %collective-permute-start.6 = (bf16[72,128]{1,0:T(8,128)(2,1)S(1)}, bf16[72,128]{1,0:T(8,128)(2,1)S(1)}, u32[]{:S(2)}, u32[]{:S(2)}) collective-permute-start(bf16[72,128]{1,0:T(8,128)(2,1)S(1)} %collective-permute-done.3.refs_3_), channel_id=1, source_target_pairs={{0,1},{1,0},{2,3},{3,2},{4,5},{5,4},{6,7},{7,6},{8,9},{9,8},{10,11... | collective-permute-start | bytes 55304 | tf_op jit(solution)/shard_map/ppermute | solution.py:125
  26.5 0.0 collective-permute-done.2.refs_2_
  26.5 0.7 %collective-permute-start.5 = (bf16[72,128]{1,0:T(8,128)(2,1)S(1)}, bf16[72,128]{1,0:T(8,128)(2,1)S(1)}, u32[]{:S(2)}, u32[]{:S(2)}) collective-permute-start(bf16[72,128]{1,0:T(8,128)(2,1)S(1)} %collective-permute-done.2.refs_2_), channel_id=1, source_target_pairs={{0,1},{1,0},{2,3},{3,2},{4,5},{5,4},{6,7},{7,6},{8,9},{9,8},{10,11... | collective-permute-start | bytes 55304 | tf_op jit(solution)/shard_map/ppermute | solution.py:125
  27.2 0.4 %collective-permute-done.1.refs_1_ = bf16[72,128]{1,0:T(8,128)(2,1)S(1)} collective-permute-done((bf16[72,128]{1,0:T(8,128)(2,1)S(1)}, bf16[72,128]{1,0:T(8,128)(2,1)S(1)}, u32[]{:S(2)}, u32[]{:S(2)}) %collective-permute-start.1) | collective-permute-done | bytes 18464 | tf_op jit(solution)/shard_map/ppermute | solution.py:125
  27.5 0.0 collective-permute-done.7.refs_7_
  27.5 0.0 collective-permute-done.6.refs_6_
  27.5 0.5 %collective-permute-done.5.refs_5_ = bf16[72,128]{1,0:T(8,128)(2,1)S(1)} collective-permute-done((bf16[72,128]{1,0:T(8,128)(2,1)S(1)}, bf16[72,128]{1,0:T(8,128)(2,1)S(1)}, u32[]{:S(2)}, u32[]{:S(2)}) %collective-permute-start.5) | collective-permute-done | bytes 18464 | tf_op jit(solution)/shard_map/ppermute | solution.py:125
  28.0 1.2 %shard_map.51 = (bf16[8,64]{1,0:T(8,128)(2,1)}, f32[64,64]{1,0:T(8,128)}) custom-call(bf16[72,128]{1,0:T(8,128)(2,1)S(1)} %add_convert_fusion.refs_0_, bf16[72,128]{1,0:T(8,128)(2,1)S(1)} %collective-permute-done.1.refs_1_, bf16[72,128]{1,0:T(8,128)(2,1)S(1)} %collective-permute-done.2.refs_2_, bf16[72,128]{1,0:T(8,128)(2,1)S(1)} %collective-permute-done.3.refs_3_, ...), custom_call_target="tpu_custom_call" | custom-call | tf_op jit(solution)/shard_map/pallas_call | solution.py:159
  (1 shorter events, 0.0 us)
Async XLA Ops:
  18.9 1.3 %collective-permute-start = (f32[72,128]{1,0:T(8,128)S(1)}, f32[72,128]{1,0:T(8,128)S(1)}, u32[]{:S(2)}, u32[]{:S(2)}) collective-permute-start(f32[72,128]{1,0:T(8,128)S(1)} %shard_map.50), channel_id=1, source_target_pairs={{0,1},{1,0},{2,3},{3,2},{4,5},{5,4},{6,7},{7,6},{8,9},{9,8},{10,11... | collective-permute-start | bytes 110600 | tf_op jit(solution)/shard_map/ppermute | solution.py:125
  20.1 5.8 %collective-permute-start.4 = (bf16[72,128]{1,0:T(8,128)(2,1)S(1)}, bf16[72,128]{1,0:T(8,128)(2,1)S(1)}, u32[]{:S(2)}, u32[]{:S(2)}) collective-permute-start(bf16[72,128]{1,0:T(8,128)(2,1)S(1)} %add_convert_fusion.refs_0_), channel_id=1, source_target_pairs={{0,10},{1,15},{2,8},{3,13},{4,14},{5,11},{6,12},{7,9},{8,2},{9,7},... | collective-permute-start | bytes 55304 | tf_op jit(solution)/shard_map/ppermute | solution.py:125
  20.4 5.6 %collective-permute-start.3 = (bf16[72,128]{1,0:T(8,128)(2,1)S(1)}, bf16[72,128]{1,0:T(8,128)(2,1)S(1)}, u32[]{:S(2)}, u32[]{:S(2)}) collective-permute-start(bf16[72,128]{1,0:T(8,128)(2,1)S(1)} %add_convert_fusion.refs_0_), channel_id=1, source_target_pairs={{0,8},{1,13},{2,10},{3,15},{4,12},{5,9},{6,14},{7,11},{8,0},{9,5},... | collective-permute-start | bytes 55304 | tf_op jit(solution)/shard_map/ppermute | solution.py:125
  22.7 3.8 %collective-permute-start.2 = (bf16[72,128]{1,0:T(8,128)(2,1)S(1)}, bf16[72,128]{1,0:T(8,128)(2,1)S(1)}, u32[]{:S(2)}, u32[]{:S(2)}) collective-permute-start(bf16[72,128]{1,0:T(8,128)(2,1)S(1)} %add_convert_fusion.refs_0_), channel_id=1, source_target_pairs={{0,4},{1,7},{2,6},{3,5},{4,0},{5,3},{6,2},{7,1},{8,12},{9,15},{10,... | collective-permute-start | bytes 55304 | tf_op jit(solution)/shard_map/ppermute | solution.py:125
  23.7 3.8 %collective-permute-start.1 = (bf16[72,128]{1,0:T(8,128)(2,1)S(1)}, bf16[72,128]{1,0:T(8,128)(2,1)S(1)}, u32[]{:S(2)}, u32[]{:S(2)}) collective-permute-start(bf16[72,128]{1,0:T(8,128)(2,1)S(1)} %add_convert_fusion.refs_0_), channel_id=1, source_target_pairs={{0,2},{1,3},{2,0},{3,1},{4,6},{5,7},{6,4},{7,5},{8,10},{9,11},{10,... | collective-permute-start | bytes 55304 | tf_op jit(solution)/shard_map/ppermute | solution.py:125
  26.0 1.6 %collective-permute-start.7 = (bf16[72,128]{1,0:T(8,128)(2,1)S(1)}, bf16[72,128]{1,0:T(8,128)(2,1)S(1)}, u32[]{:S(2)}, u32[]{:S(2)}) collective-permute-start(bf16[72,128]{1,0:T(8,128)(2,1)S(1)} %collective-permute-done.4.refs_4_), channel_id=1, source_target_pairs={{0,1},{1,0},{2,3},{3,2},{4,5},{5,4},{6,7},{7,6},{8,9},{9,8},{10,11... | collective-permute-start | bytes 55304 | tf_op jit(solution)/shard_map/ppermute | solution.py:125
  26.0 1.6 %collective-permute-start.6 = (bf16[72,128]{1,0:T(8,128)(2,1)S(1)}, bf16[72,128]{1,0:T(8,128)(2,1)S(1)}, u32[]{:S(2)}, u32[]{:S(2)}) collective-permute-start(bf16[72,128]{1,0:T(8,128)(2,1)S(1)} %collective-permute-done.3.refs_3_), channel_id=1, source_target_pairs={{0,1},{1,0},{2,3},{3,2},{4,5},{5,4},{6,7},{7,6},{8,9},{9,8},{10,11... | collective-permute-start | bytes 55304 | tf_op jit(solution)/shard_map/ppermute | solution.py:125
  26.5 1.5 %collective-permute-start.5 = (bf16[72,128]{1,0:T(8,128)(2,1)S(1)}, bf16[72,128]{1,0:T(8,128)(2,1)S(1)}, u32[]{:S(2)}, u32[]{:S(2)}) collective-permute-start(bf16[72,128]{1,0:T(8,128)(2,1)S(1)} %collective-permute-done.2.refs_2_), channel_id=1, source_target_pairs={{0,1},{1,0},{2,3},{3,2},{4,5},{5,4},{6,7},{7,6},{8,9},{9,8},{10,11... | collective-permute-start | bytes 55304 | tf_op jit(solution)/shard_map/ppermute | solution.py:125

commit v7 on v6

--- a/solution.py
+++ b/solution.py
@@ -10,13 +10,9 @@
 CORES = 2
 
 
-def partial_kernel(features_ref, basis_hbm, density_hbm, message_ref, basis_ref, density_ref, sems):
-    copies = [
-        pltpu.make_async_copy(basis_hbm, basis_ref, sems.at[0]),
-        pltpu.make_async_copy(density_hbm, density_ref, sems.at[1]),
-    ]
-    for copy in copies:
-        copy.start()
+def partial_kernel(features_ref, basis_ref, density_hbm, message_ref, density_ref, sem):
+    copy = pltpu.make_async_copy(density_hbm, density_ref, sem)
+    copy.start()
     features = features_ref[...]
     total = features.shape[0]
     half = total // 2
@@ -36,8 +32,7 @@
     own_row, own_lane = row[:half], lane[:half]
     packed = jnp.where((own_lane < half) & (own_row >= own_lane), bottom, top)
 
-    for copy in copies:
-        copy.wait()
+    copy.wait()
     me = lax.axis_index("blk")
     density = density_ref[...].astype(jnp.float32).reshape(1, rows)
     density = jnp.concatenate([density, jnp.zeros((1, total - rows), jnp.float32)], axis=1)
@@ -50,9 +45,14 @@
 
 
 def routes(pairs):
-    half, quarter = pairs // 2, pairs // 4
-    near = [(offset, offset + 1) for offset in range(2, half, 2)]
-    return [(1, 1)] + near + [(half + step, half + quarter + step) for step in range(quarter)]
+    half = pairs // 2
+    near = [(1, 3)] + [(offset, offset + 1) for offset in range(4, half, 2)]
+    far = [
+        step
+        for base in range(half, pairs, 4)
+        for step in ((base, base + 3), (base + 2, base + 1))
+    ]
+    return [(2, 2)] + near + far
 
 
 def pieces(value):
@@ -136,17 +136,16 @@
     partial = pl.pallas_call(
         partial_kernel,
         out_shape=jax.ShapeDtypeStruct((total // 2 + rows, total), jnp.float32),
-        in_specs=[whole] + [pl.BlockSpec(memory_space=pltpu.HBM)] * 2,
+        in_specs=[whole] * 2 + [pl.BlockSpec(memory_space=pltpu.HBM)],
         out_specs=whole,
         scratch_shapes=[
-            pltpu.VMEM(basis.shape, basis.dtype),
             pltpu.VMEM(density.shape, density.dtype),
-            pltpu.SemaphoreType.DMA((2,)),
+            pltpu.SemaphoreType.DMA(()),
         ],
         compiler_params=params,
     )(
         features,
-        pltpu.with_memory_space_constraint(basis, pltpu.HBM),
+        basis,
         pltpu.with_memory_space_constraint(density, pltpu.HBM),
     )
     sibling = (1, 1)

time: 29.4 us -> 29.4 us (level)
  starting transfers between devices: 6 us -> 5.63 us
  waiting for transfers between devices: 3.11 us -> 3.47 us
    ppermute x8, starting transfers between devices: 6 us -> 5.63 us  [from_peer(): lax.ppermute(value, 'blk', [(i, i ^ offsets[i % CORES]) for i in range(co...]
    ppermute x8, waiting for transfers between devices: 3.11 us -> 3.47 us  [from_peer(): lax.ppermute(value, 'blk', [(i, i ^ offsets[i % CORES]) for i in range(co...]
  transfers between devices with their start and end apart: 8 -> 8, of which waited for: 4 -> 5; matrix products, arithmetic and copies ran while one was open for 0% -> 0% of each run, Pallas kernels for 0% -> 0%
where the time goes in v7:
time: 29.4 us; the launch traced here: 29.1 us
  blocking collectives  17.4 us (59%)
  starting transfers between devices  5.63 us (19%)
  waiting for transfers between devices  3.47 us (12%)
  Pallas kernels  1.89 us (6%)
  between operations  0.67 us (2%)
    all_to_all x1, blocking collectives, shards(): lax.all_to_all(frames, 'blk', split_axis=1, concat_axis=0, tiled=True)  17.4 us
    ppermute x8, starting transfers between devices, from_peer(): lax.ppermute(value, 'blk', [(i, i ^ offsets[i % CORES]) for i in range(co...  5.63 us
    ppermute x8, waiting for transfers between devices, from_peer(): lax.ppermute(value, 'blk', [(i, i ^ offsets[i % CORES]) for i in range(co...  3.47 us
    pallas_call x1, Pallas kernels, shards(): pl.pallas_call(functools.partial(finish_kernel, feature_count, width, row...  1.15 us
    pallas_call x1, Pallas kernels, shards(): pl.pallas_call(partial_kernel, out_shape=jax.ShapeDtypeStruct((total // 2...  0.74 us
  transfers between devices with their start and end apart: 8, of which 5 were waited for; matrix products, arithmetic and copies ran while one was open for 0% of the time, Pallas kernels for 0%

profile of v7, /device:TPU:0, one launch (start us, length us, event | category | flops | bytes accessed | tf_op | source)
XLA Modules:
  0.0 29.1 jit_solution(93515803749027213)
XLA Ops:
  0.6 0.0 copy-start
  0.6 17.4 %all_to_all.19 = bf16[8,16,1024]{2,0,1:T(8,128)(2,1)S(1)} all-to-all(bf16[8,16,1024]{2,0,1:T(8,128)(2,1)} %bitcast.5), channel_id=1, replica_groups=mesh['groups'=2,'blk'=16] {'blk'}, dimensions={1} | all-to-all | bytes 524288 | tf_op jit(solution)/shard_map/all_to_all | solution.py:135
  18.1 0.0 copy-done
  18.1 0.7 %shard_map.50 = f32[72,128]{1,0:T(8,128)S(1)} custom-call(bf16[128,1024]{1,0:T(8,128)(2,1)S(1)} %bitcast.4, bf16[8,64]{1,0:T(8,128)(2,1)S(1)} %copy-done, bf16[8]{0:T(256)(128)(2,1)} %density_hbm.1), custom_call_target="tpu_custom_call" | custom-call | tf_op jit(solution)/shard_map/pallas_call | solution.py:136
  18.8 0.1 collective-permute-start
  18.9 1.2 %collective-permute-done = f32[72,128]{1,0:T(8,128)S(1)} collective-permute-done((f32[72,128]{1,0:T(8,128)S(1)}, f32[72,128]{1,0:T(8,128)S(1)}, u32[]{:S(2)}, u32[]{:S(2)}) %collective-permute-start) | collective-permute-done | bytes 36896 | tf_op jit(solution)/shard_map/ppermute | solution.py:125
  20.1 1.1 %collective-permute-start.4 = (bf16[72,128]{1,0:T(8,128)(2,1)S(1)}, bf16[72,128]{1,0:T(8,128)(2,1)S(1)}, u32[]{:S(2)}, u32[]{:S(2)}) collective-permute-start(bf16[72,128]{1,0:T(8,128)(2,1)S(1)} %add_convert_fusion.refs_0_), channel_id=1, source_target_pairs={{0,12},{1,11},{2,14},{3,9},{4,8},{5,15},{6,10},{7,13},{8,4},{9,3},... | collective-permute-start | bytes 55304 | tf_op jit(solution)/shard_map/ppermute | solution.py:125
  21.2 0.8 %collective-permute-start.3 = (bf16[72,128]{1,0:T(8,128)(2,1)S(1)}, bf16[72,128]{1,0:T(8,128)(2,1)S(1)}, u32[]{:S(2)}, u32[]{:S(2)}) collective-permute-start(bf16[72,128]{1,0:T(8,128)(2,1)S(1)} %add_convert_fusion.refs_0_), channel_id=1, source_target_pairs={{0,8},{1,15},{2,10},{3,13},{4,12},{5,11},{6,14},{7,9},{8,0},{9,7},... | collective-permute-start | bytes 55304 | tf_op jit(solution)/shard_map/ppermute | solution.py:125
  22.0 0.8 %collective-permute-start.2 = (bf16[72,128]{1,0:T(8,128)(2,1)S(1)}, bf16[72,128]{1,0:T(8,128)(2,1)S(1)}, u32[]{:S(2)}, u32[]{:S(2)}) collective-permute-start(bf16[72,128]{1,0:T(8,128)(2,1)S(1)} %add_convert_fusion.refs_0_), channel_id=1, source_target_pairs={{0,2},{1,7},{2,0},{3,5},{4,6},{5,3},{6,4},{7,1},{8,10},{9,15},{10,... | collective-permute-start | bytes 55304 | tf_op jit(solution)/shard_map/ppermute | solution.py:125
  22.8 1.9 %collective-permute-start.1 = (bf16[72,128]{1,0:T(8,128)(2,1)S(1)}, bf16[72,128]{1,0:T(8,128)(2,1)S(1)}, u32[]{:S(2)}, u32[]{:S(2)}) collective-permute-start(bf16[72,128]{1,0:T(8,128)(2,1)S(1)} %add_convert_fusion.refs_0_), channel_id=1, source_target_pairs={{0,4},{1,5},{2,6},{3,7},{4,0},{5,1},{6,2},{7,3},{8,12},{9,13},{10,... | collective-permute-start | bytes 55304 | tf_op jit(solution)/shard_map/ppermute | solution.py:125
  24.7 1.0 %collective-permute-done.4.refs_4_ = bf16[72,128]{1,0:T(8,128)(2,1)S(1)} collective-permute-done((bf16[72,128]{1,0:T(8,128)(2,1)S(1)}, bf16[72,128]{1,0:T(8,128)(2,1)S(1)}, u32[]{:S(2)}, u32[]{:S(2)}) %collective-permute-start.4) | collective-permute-done | bytes 18464 | tf_op jit(solution)/shard_map/ppermute | solution.py:125
  25.8 0.0 collective-permute-start.7
  25.8 0.4 %collective-permute-done.3.refs_3_ = bf16[72,128]{1,0:T(8,128)(2,1)S(1)} collective-permute-done((bf16[72,128]{1,0:T(8,128)(2,1)S(1)}, bf16[72,128]{1,0:T(8,128)(2,1)S(1)}, u32[]{:S(2)}, u32[]{:S(2)}) %collective-permute-start.3) | collective-permute-done | bytes 18464 | tf_op jit(solution)/shard_map/ppermute | solution.py:125
  26.1 0.1 collective-permute-start.6
  26.3 0.0 collective-permute-done.2.refs_2_
  26.3 0.8 %collective-permute-start.5 = (bf16[72,128]{1,0:T(8,128)(2,1)S(1)}, bf16[72,128]{1,0:T(8,128)(2,1)S(1)}, u32[]{:S(2)}, u32[]{:S(2)}) collective-permute-start(bf16[72,128]{1,0:T(8,128)(2,1)S(1)} %collective-permute-done.2.refs_2_), channel_id=1, source_target_pairs={{0,1},{1,0},{2,3},{3,2},{4,5},{5,4},{6,7},{7,6},{8,9},{9,8},{10,11... | collective-permute-start | bytes 55304 | tf_op jit(solution)/shard_map/ppermute | solution.py:125
  27.1 0.0 collective-permute-done.1.refs_1_
  27.1 0.0 collective-permute-done.7.refs_7_
  27.1 0.2 collective-permute-done.6.refs_6_
  27.3 0.6 %collective-permute-done.5.refs_5_ = bf16[72,128]{1,0:T(8,128)(2,1)S(1)} collective-permute-done((bf16[72,128]{1,0:T(8,128)(2,1)S(1)}, bf16[72,128]{1,0:T(8,128)(2,1)S(1)}, u32[]{:S(2)}, u32[]{:S(2)}) %collective-permute-start.5) | collective-permute-done | bytes 18464 | tf_op jit(solution)/shard_map/ppermute | solution.py:125
  28.0 1.2 %shard_map.51 = (bf16[8,64]{1,0:T(8,128)(2,1)}, f32[64,64]{1,0:T(8,128)}) custom-call(bf16[72,128]{1,0:T(8,128)(2,1)S(1)} %add_convert_fusion.refs_0_, bf16[72,128]{1,0:T(8,128)(2,1)S(1)} %collective-permute-done.1.refs_1_, bf16[72,128]{1,0:T(8,128)(2,1)S(1)} %collective-permute-done.2.refs_2_, bf16[72,128]{1,0:T(8,128)(2,1)S(1)} %collective-permute-done.3.refs_3_, ...), custom_call_target="tpu_custom_call" | custom-call | tf_op jit(solution)/shard_map/pallas_call | solution.py:158
  (1 shorter events, 0.0 us)
Async XLA Ops:
  0.6 17.5 %copy-start = (bf16[8,64]{1,0:T(8,128)(2,1)S(1)}, bf16[8,64]{1,0:T(8,128)(2,1)}, u32[]{:S(2)}) copy-start(bf16[8,64]{1,0:T(8,128)(2,1)} %basis_ref.1) | copy-start | bytes 3076
  18.8 1.3 %collective-permute-start = (f32[72,128]{1,0:T(8,128)S(1)}, f32[72,128]{1,0:T(8,128)S(1)}, u32[]{:S(2)}, u32[]{:S(2)}) collective-permute-start(f32[72,128]{1,0:T(8,128)S(1)} %shard_map.50), channel_id=1, source_target_pairs={{0,1},{1,0},{2,3},{3,2},{4,5},{5,4},{6,7},{7,6},{8,9},{9,8},{10,11... | collective-permute-start | bytes 110600 | tf_op jit(solution)/shard_map/ppermute | solution.py:125
  20.1 5.6 %collective-permute-start.4 = (bf16[72,128]{1,0:T(8,128)(2,1)S(1)}, bf16[72,128]{1,0:T(8,128)(2,1)S(1)}, u32[]{:S(2)}, u32[]{:S(2)}) collective-permute-start(bf16[72,128]{1,0:T(8,128)(2,1)S(1)} %add_convert_fusion.refs_0_), channel_id=1, source_target_pairs={{0,12},{1,11},{2,14},{3,9},{4,8},{5,15},{6,10},{7,13},{8,4},{9,3},... | collective-permute-start | bytes 55304 | tf_op jit(solution)/shard_map/ppermute | solution.py:125
  21.2 5.0 %collective-permute-start.3 = (bf16[72,128]{1,0:T(8,128)(2,1)S(1)}, bf16[72,128]{1,0:T(8,128)(2,1)S(1)}, u32[]{:S(2)}, u32[]{:S(2)}) collective-permute-start(bf16[72,128]{1,0:T(8,128)(2,1)S(1)} %add_convert_fusion.refs_0_), channel_id=1, source_target_pairs={{0,8},{1,15},{2,10},{3,13},{4,12},{5,11},{6,14},{7,9},{8,0},{9,7},... | collective-permute-start | bytes 55304 | tf_op jit(solution)/shard_map/ppermute | solution.py:125
  22.0 4.3 %collective-permute-start.2 = (bf16[72,128]{1,0:T(8,128)(2,1)S(1)}, bf16[72,128]{1,0:T(8,128)(2,1)S(1)}, u32[]{:S(2)}, u32[]{:S(2)}) collective-permute-start(bf16[72,128]{1,0:T(8,128)(2,1)S(1)} %add_convert_fusion.refs_0_), channel_id=1, source_target_pairs={{0,2},{1,7},{2,0},{3,5},{4,6},{5,3},{6,4},{7,1},{8,10},{9,15},{10,... | collective-permute-start | bytes 55304 | tf_op jit(solution)/shard_map/ppermute | solution.py:125
  22.8 4.3 %collective-permute-start.1 = (bf16[72,128]{1,0:T(8,128)(2,1)S(1)}, bf16[72,128]{1,0:T(8,128)(2,1)S(1)}, u32[]{:S(2)}, u32[]{:S(2)}) collective-permute-start(bf16[72,128]{1,0:T(8,128)(2,1)S(1)} %add_convert_fusion.refs_0_), channel_id=1, source_target_pairs={{0,4},{1,5},{2,6},{3,7},{4,0},{5,1},{6,2},{7,3},{8,12},{9,13},{10,... | collective-permute-start | bytes 55304 | tf_op jit(solution)/shard_map/ppermute | solution.py:125
  25.8 1.4 %collective-permute-start.7 = (bf16[72,128]{1,0:T(8,128)(2,1)S(1)}, bf16[72,128]{1,0:T(8,128)(2,1)S(1)}, u32[]{:S(2)}, u32[]{:S(2)}) collective-permute-start(bf16[72,128]{1,0:T(8,128)(2,1)S(1)} %collective-permute-done.4.refs_4_), channel_id=1, source_target_pairs={{0,1},{1,0},{2,3},{3,2},{4,5},{5,4},{6,7},{7,6},{8,9},{9,8},{10,11... | collective-permute-start | bytes 55304 | tf_op jit(solution)/shard_map/ppermute | solution.py:125
  26.1 1.2 %collective-permute-start.6 = (bf16[72,128]{1,0:T(8,128)(2,1)S(1)}, bf16[72,128]{1,0:T(8,128)(2,1)S(1)}, u32[]{:S(2)}, u32[]{:S(2)}) collective-permute-start(bf16[72,128]{1,0:T(8,128)(2,1)S(1)} %collective-permute-done.3.refs_3_), channel_id=1, source_target_pairs={{0,1},{1,0},{2,3},{3,2},{4,5},{5,4},{6,7},{7,6},{8,9},{9,8},{10,11... | collective-permute-start | bytes 55304 | tf_op jit(solution)/shard_map/ppermute | solution.py:125
  26.3 1.7 %collective-permute-start.5 = (bf16[72,128]{1,0:T(8,128)(2,1)S(1)}, bf16[72,128]{1,0:T(8,128)(2,1)S(1)}, u32[]{:S(2)}, u32[]{:S(2)}) collective-permute-start(bf16[72,128]{1,0:T(8,128)(2,1)S(1)} %collective-permute-done.2.refs_2_), channel_id=1, source_target_pairs={{0,1},{1,0},{2,3},{3,2},{4,5},{5,4},{6,7},{7,6},{8,9},{9,8},{10,11... | collective-permute-start | bytes 55304 | tf_op jit(solution)/shard_map/ppermute | solution.py:125

commit v8 on v7

--- a/solution.py
+++ b/solution.py
@@ -71,6 +71,24 @@
     core, pair = lax.rem(me, CORES), lax.div(me, CORES)
     steps = routes(pairs)
     steps = steps + [(two, one) for one, two in steps[1:]]
+    for step, ref in zip(steps + [(0, 0)], message_refs + [own_ref]):
+        both = ref[half:].astype(jnp.float32)
+        base = (pair ^ jnp.where(core == 0, step[0], step[1])) * CORES * rows
+        for place in range(CORES):
+            block = both[:, place * width : (place + 1) * width]
+            vectors_ref[pl.ds(pl.multiple_of(base + place * rows, rows), rows), :] = block
+    vectors = vectors_ref[...]
+    own_rows = pl.ds(pl.multiple_of(me * rows, rows), rows)
+    extended = jnp.concatenate(
+        [vectors, jnp.ones((total, 1), jnp.float32), jnp.zeros((total, width - 1), jnp.float32)], axis=1
+    )
+    overlaps = lax.dot_general(
+        vectors_ref[own_rows, :].astype(jnp.bfloat16),
+        vectors.astype(jnp.bfloat16),
+        (((1,), (1,)), ((), ())),
+        preferred_element_type=jnp.float32,
+    )
+    left = jnp.concatenate([vectors.T, *pieces(overlaps)], axis=0).astype(jnp.bfloat16)
     near = own_ref[:half].astype(jnp.float32)
     far = jnp.zeros_like(near)
     for step, ref in zip(steps, message_refs):
@@ -91,24 +109,6 @@
     one_side = jnp.concatenate([top, bottom], axis=0)
     dist = one_side + one_side.T
     weight = (jnp.exp(-dist / feature_count) * density).astype(jnp.bfloat16)
-    for step, ref in zip(steps + [(0, 0)], message_refs + [own_ref]):
-        both = ref[half:].astype(jnp.float32)
-        base = (pair ^ jnp.where(core == 0, step[0], step[1])) * CORES * rows
-        for place in range(CORES):
-            block = both[:, place * width : (place + 1) * width]
-            vectors_ref[pl.ds(pl.multiple_of(base + place * rows, rows), rows), :] = block
-    vectors = vectors_ref[...]
-    own_rows = pl.ds(pl.multiple_of(me * rows, rows), rows)
-    extended = jnp.concatenate(
-        [vectors, jnp.ones((total, 1), jnp.float32), jnp.zeros((total, width - 1), jnp.float32)], axis=1
-    )
-    overlaps = lax.dot_general(
-        vectors_ref[own_rows, :].astype(jnp.bfloat16),
-        vectors.astype(jnp.bfloat16),
-        (((1,), (1,)), ((), ())),
-        preferred_element_type=jnp.float32,
-    )
-    left = jnp.concatenate([vectors.T, *pieces(overlaps)], axis=0).astype(jnp.bfloat16)
     numer = jnp.dot(weight, extended.astype(jnp.bfloat16), preferred_element_type=jnp.float32)
     applied = numer[:, :width] / numer[:, width : width + 1]
     applied_ref[...] = applied

time: 29.4 us -> 29.4 us (level)
  no operation moved by 1% of the time
where the time goes in v8:
time: 29.4 us; the launch traced here: 29.1 us
  blocking collectives  17.4 us (59%)
  starting transfers between devices  5.63 us (19%)
  waiting for transfers between devices  3.47 us (12%)
  Pallas kernels  1.89 us (6%)
  between operations  0.67 us (2%)
    all_to_all x1, blocking collectives, shards(): lax.all_to_all(frames, 'blk', split_axis=1, concat_axis=0, tiled=True)  17.4 us
    ppermute x8, starting transfers between devices, from_peer(): lax.ppermute(value, 'blk', [(i, i ^ offsets[i % CORES]) for i in range(co...  5.63 us
    ppermute x8, waiting for transfers between devices, from_peer(): lax.ppermute(value, 'blk', [(i, i ^ offsets[i % CORES]) for i in range(co...  3.47 us
    pallas_call x1, Pallas kernels, shards(): pl.pallas_call(functools.partial(finish_kernel, feature_count, width, row...  1.15 us
    pallas_call x1, Pallas kernels, shards(): pl.pallas_call(partial_kernel, out_shape=jax.ShapeDtypeStruct((total // 2...  0.74 us
  transfers between devices with their start and end apart: 8, of which 5 were waited for; matrix products, arithmetic and copies ran while one was open for 0% of the time, Pallas kernels for 0%

profile of v8, /device:TPU:0, one launch (start us, length us, event | category | flops | bytes accessed | tf_op | source)
XLA Modules:
  0.0 29.1 jit_solution(9996224043719351996)
XLA Ops:
  0.6 0.0 copy-start
  0.6 17.4 %all_to_all.19 = bf16[8,16,1024]{2,0,1:T(8,128)(2,1)S(1)} all-to-all(bf16[8,16,1024]{2,0,1:T(8,128)(2,1)} %bitcast.5), channel_id=1, replica_groups=mesh['groups'=2,'blk'=16] {'blk'}, dimensions={1} | all-to-all | bytes 524288 | tf_op jit(solution)/shard_map/all_to_all | solution.py:135
  18.1 0.0 copy-done
  18.1 0.7 %shard_map.50 = f32[72,128]{1,0:T(8,128)S(1)} custom-call(bf16[128,1024]{1,0:T(8,128)(2,1)S(1)} %bitcast.4, bf16[8,64]{1,0:T(8,128)(2,1)S(1)} %copy-done, bf16[8]{0:T(256)(128)(2,1)} %density_hbm.1), custom_call_target="tpu_custom_call" | custom-call | tf_op jit(solution)/shard_map/pallas_call | solution.py:136
  18.8 0.1 collective-permute-start
  18.9 1.2 %collective-permute-done = f32[72,128]{1,0:T(8,128)S(1)} collective-permute-done((f32[72,128]{1,0:T(8,128)S(1)}, f32[72,128]{1,0:T(8,128)S(1)}, u32[]{:S(2)}, u32[]{:S(2)}) %collective-permute-start) | collective-permute-done | bytes 36896 | tf_op jit(solution)/shard_map/ppermute | solution.py:125
  20.1 1.1 %collective-permute-start.4 = (bf16[72,128]{1,0:T(8,128)(2,1)S(1)}, bf16[72,128]{1,0:T(8,128)(2,1)S(1)}, u32[]{:S(2)}, u32[]{:S(2)}) collective-permute-start(bf16[72,128]{1,0:T(8,128)(2,1)S(1)} %add_convert_fusion.refs_0_), channel_id=1, source_target_pairs={{0,12},{1,11},{2,14},{3,9},{4,8},{5,15},{6,10},{7,13},{8,4},{9,3},... | collective-permute-start | bytes 55304 | tf_op jit(solution)/shard_map/ppermute | solution.py:125
  21.2 0.8 %collective-permute-start.3 = (bf16[72,128]{1,0:T(8,128)(2,1)S(1)}, bf16[72,128]{1,0:T(8,128)(2,1)S(1)}, u32[]{:S(2)}, u32[]{:S(2)}) collective-permute-start(bf16[72,128]{1,0:T(8,128)(2,1)S(1)} %add_convert_fusion.refs_0_), channel_id=1, source_target_pairs={{0,8},{1,15},{2,10},{3,13},{4,12},{5,11},{6,14},{7,9},{8,0},{9,7},... | collective-permute-start | bytes 55304 | tf_op jit(solution)/shard_map/ppermute | solution.py:125
  22.0 0.8 %collective-permute-start.2 = (bf16[72,128]{1,0:T(8,128)(2,1)S(1)}, bf16[72,128]{1,0:T(8,128)(2,1)S(1)}, u32[]{:S(2)}, u32[]{:S(2)}) collective-permute-start(bf16[72,128]{1,0:T(8,128)(2,1)S(1)} %add_convert_fusion.refs_0_), channel_id=1, source_target_pairs={{0,2},{1,7},{2,0},{3,5},{4,6},{5,3},{6,4},{7,1},{8,10},{9,15},{10,... | collective-permute-start | bytes 55304 | tf_op jit(solution)/shard_map/ppermute | solution.py:125
  22.8 1.9 %collective-permute-start.1 = (bf16[72,128]{1,0:T(8,128)(2,1)S(1)}, bf16[72,128]{1,0:T(8,128)(2,1)S(1)}, u32[]{:S(2)}, u32[]{:S(2)}) collective-permute-start(bf16[72,128]{1,0:T(8,128)(2,1)S(1)} %add_convert_fusion.refs_0_), channel_id=1, source_target_pairs={{0,4},{1,5},{2,6},{3,7},{4,0},{5,1},{6,2},{7,3},{8,12},{9,13},{10,... | collective-permute-start | bytes 55304 | tf_op jit(solution)/shard_map/ppermute | solution.py:125
  24.7 1.0 %collective-permute-done.4.refs_4_ = bf16[72,128]{1,0:T(8,128)(2,1)S(1)} collective-permute-done((bf16[72,128]{1,0:T(8,128)(2,1)S(1)}, bf16[72,128]{1,0:T(8,128)(2,1)S(1)}, u32[]{:S(2)}, u32[]{:S(2)}) %collective-permute-start.4) | collective-permute-done | bytes 18464 | tf_op jit(solution)/shard_map/ppermute | solution.py:125
  25.8 0.0 collective-permute-start.7
  25.8 0.4 %collective-permute-done.3.refs_3_ = bf16[72,128]{1,0:T(8,128)(2,1)S(1)} collective-permute-done((bf16[72,128]{1,0:T(8,128)(2,1)S(1)}, bf16[72,128]{1,0:T(8,128)(2,1)S(1)}, u32[]{:S(2)}, u32[]{:S(2)}) %collective-permute-start.3) | collective-permute-done | bytes 18464 | tf_op jit(solution)/shard_map/ppermute | solution.py:125
  26.1 0.1 collective-permute-start.6
  26.3 0.0 collective-permute-done.2.refs_2_
  26.3 0.8 %collective-permute-start.5 = (bf16[72,128]{1,0:T(8,128)(2,1)S(1)}, bf16[72,128]{1,0:T(8,128)(2,1)S(1)}, u32[]{:S(2)}, u32[]{:S(2)}) collective-permute-start(bf16[72,128]{1,0:T(8,128)(2,1)S(1)} %collective-permute-done.2.refs_2_), channel_id=1, source_target_pairs={{0,1},{1,0},{2,3},{3,2},{4,5},{5,4},{6,7},{7,6},{8,9},{9,8},{10,11... | collective-permute-start | bytes 55304 | tf_op jit(solution)/shard_map/ppermute | solution.py:125
  27.1 0.0 collective-permute-done.1.refs_1_
  27.1 0.0 collective-permute-done.7.refs_7_
  27.1 0.2 collective-permute-done.6.refs_6_
  27.3 0.6 %collective-permute-done.5.refs_5_ = bf16[72,128]{1,0:T(8,128)(2,1)S(1)} collective-permute-done((bf16[72,128]{1,0:T(8,128)(2,1)S(1)}, bf16[72,128]{1,0:T(8,128)(2,1)S(1)}, u32[]{:S(2)}, u32[]{:S(2)}) %collective-permute-start.5) | collective-permute-done | bytes 18464 | tf_op jit(solution)/shard_map/ppermute | solution.py:125
  28.0 1.2 %shard_map.51 = (bf16[8,64]{1,0:T(8,128)(2,1)}, f32[64,64]{1,0:T(8,128)}) custom-call(bf16[72,128]{1,0:T(8,128)(2,1)S(1)} %add_convert_fusion.refs_0_, bf16[72,128]{1,0:T(8,128)(2,1)S(1)} %collective-permute-done.1.refs_1_, bf16[72,128]{1,0:T(8,128)(2,1)S(1)} %collective-permute-done.2.refs_2_, bf16[72,128]{1,0:T(8,128)(2,1)S(1)} %collective-permute-done.3.refs_3_, ...), custom_call_target="tpu_custom_call" | custom-call | tf_op jit(solution)/shard_map/pallas_call | solution.py:158
  (1 shorter events, 0.0 us)
Async XLA Ops:
  0.6 17.5 %copy-start = (bf16[8,64]{1,0:T(8,128)(2,1)S(1)}, bf16[8,64]{1,0:T(8,128)(2,1)}, u32[]{:S(2)}) copy-start(bf16[8,64]{1,0:T(8,128)(2,1)} %basis_ref.1) | copy-start | bytes 3076
  18.8 1.3 %collective-permute-start = (f32[72,128]{1,0:T(8,128)S(1)}, f32[72,128]{1,0:T(8,128)S(1)}, u32[]{:S(2)}, u32[]{:S(2)}) collective-permute-start(f32[72,128]{1,0:T(8,128)S(1)} %shard_map.50), channel_id=1, source_target_pairs={{0,1},{1,0},{2,3},{3,2},{4,5},{5,4},{6,7},{7,6},{8,9},{9,8},{10,11... | collective-permute-start | bytes 110600 | tf_op jit(solution)/shard_map/ppermute | solution.py:125
  20.1 5.6 %collective-permute-start.4 = (bf16[72,128]{1,0:T(8,128)(2,1)S(1)}, bf16[72,128]{1,0:T(8,128)(2,1)S(1)}, u32[]{:S(2)}, u32[]{:S(2)}) collective-permute-start(bf16[72,128]{1,0:T(8,128)(2,1)S(1)} %add_convert_fusion.refs_0_), channel_id=1, source_target_pairs={{0,12},{1,11},{2,14},{3,9},{4,8},{5,15},{6,10},{7,13},{8,4},{9,3},... | collective-permute-start | bytes 55304 | tf_op jit(solution)/shard_map/ppermute | solution.py:125
  21.2 5.0 %collective-permute-start.3 = (bf16[72,128]{1,0:T(8,128)(2,1)S(1)}, bf16[72,128]{1,0:T(8,128)(2,1)S(1)}, u32[]{:S(2)}, u32[]{:S(2)}) collective-permute-start(bf16[72,128]{1,0:T(8,128)(2,1)S(1)} %add_convert_fusion.refs_0_), channel_id=1, source_target_pairs={{0,8},{1,15},{2,10},{3,13},{4,12},{5,11},{6,14},{7,9},{8,0},{9,7},... | collective-permute-start | bytes 55304 | tf_op jit(solution)/shard_map/ppermute | solution.py:125
  22.0 4.3 %collective-permute-start.2 = (bf16[72,128]{1,0:T(8,128)(2,1)S(1)}, bf16[72,128]{1,0:T(8,128)(2,1)S(1)}, u32[]{:S(2)}, u32[]{:S(2)}) collective-permute-start(bf16[72,128]{1,0:T(8,128)(2,1)S(1)} %add_convert_fusion.refs_0_), channel_id=1, source_target_pairs={{0,2},{1,7},{2,0},{3,5},{4,6},{5,3},{6,4},{7,1},{8,10},{9,15},{10,... | collective-permute-start | bytes 55304 | tf_op jit(solution)/shard_map/ppermute | solution.py:125
  22.8 4.3 %collective-permute-start.1 = (bf16[72,128]{1,0:T(8,128)(2,1)S(1)}, bf16[72,128]{1,0:T(8,128)(2,1)S(1)}, u32[]{:S(2)}, u32[]{:S(2)}) collective-permute-start(bf16[72,128]{1,0:T(8,128)(2,1)S(1)} %add_convert_fusion.refs_0_), channel_id=1, source_target_pairs={{0,4},{1,5},{2,6},{3,7},{4,0},{5,1},{6,2},{7,3},{8,12},{9,13},{10,... | collective-permute-start | bytes 55304 | tf_op jit(solution)/shard_map/ppermute | solution.py:125
  25.8 1.4 %collective-permute-start.7 = (bf16[72,128]{1,0:T(8,128)(2,1)S(1)}, bf16[72,128]{1,0:T(8,128)(2,1)S(1)}, u32[]{:S(2)}, u32[]{:S(2)}) collective-permute-start(bf16[72,128]{1,0:T(8,128)(2,1)S(1)} %collective-permute-done.4.refs_4_), channel_id=1, source_target_pairs={{0,1},{1,0},{2,3},{3,2},{4,5},{5,4},{6,7},{7,6},{8,9},{9,8},{10,11... | collective-permute-start | bytes 55304 | tf_op jit(solution)/shard_map/ppermute | solution.py:125
  26.1 1.2 %collective-permute-start.6 = (bf16[72,128]{1,0:T(8,128)(2,1)S(1)}, bf16[72,128]{1,0:T(8,128)(2,1)S(1)}, u32[]{:S(2)}, u32[]{:S(2)}) collective-permute-start(bf16[72,128]{1,0:T(8,128)(2,1)S(1)} %collective-permute-done.3.refs_3_), channel_id=1, source_target_pairs={{0,1},{1,0},{2,3},{3,2},{4,5},{5,4},{6,7},{7,6},{8,9},{9,8},{10,11... | collective-permute-start | bytes 55304 | tf_op jit(solution)/shard_map/ppermute | solution.py:125
  26.3 1.7 %collective-permute-start.5 = (bf16[72,128]{1,0:T(8,128)(2,1)S(1)}, bf16[72,128]{1,0:T(8,128)(2,1)S(1)}, u32[]{:S(2)}, u32[]{:S(2)}) collective-permute-start(bf16[72,128]{1,0:T(8,128)(2,1)S(1)} %collective-permute-done.2.refs_2_), channel_id=1, source_target_pairs={{0,1},{1,0},{2,3},{3,2},{4,5},{5,4},{6,7},{7,6},{8,9},{9,8},{10,11... | collective-permute-start | bytes 55304 | tf_op jit(solution)/shard_map/ppermute | solution.py:125
